TPU v7x, 32 devices: a whole 2x2x4 slice. The times are simulated.
32 devices in a mesh: dp: 32 (over z, y, x, core).
Axes of the slice: x: 2, y: 2, z: 4, core: 2. Of those that a mesh axis runs over, the one named last changes fastest.
Arguments:
- inputs: float32 [6144, 576], P('dp'), may hold values from -6 to 6
- cotangent: float32 [6144, 576], P('dp'), may hold values from -6 to 6
- attn_shard: bfloat16 [884736], P('dp'), may hold values from -10 to 10
- mlp_shard: bfloat16 [2654208], P('dp'), may hold values from -0.25 to 0.25
- gain_rows: float32 [2, 576], replicated, may hold values from 0.5 to 1.5
Outputs:
- outputs: float32 [6144, 576], P('dp')
- input_grad: float32 [6144, 576], P('dp')
- attn_grad: float32 [884736], P('dp')
- mlp_grad: float32 [2654208], P('dp')
- gain_grad: float32 [2, 576], replicated
All inputs are finite; a program needn't handle non-finite values.
Results may differ from a plain program's by a relative error of at most 0.014.
Values may be sent and summed in bfloat16 or wider, within the bound.
A program may use at most 128 MiB of HBM per device.

v0:
```python
import jax
import jax.numpy as jnp
from jax import lax
from jax.sharding import PartitionSpec as P

D = 576
HEADS = 9
KV_HEADS = 3
HEAD_DIM = 64
FF = 1536
SEQ_LEN = 192


EPS = 1e-05
THETA = 100000.0


def mix(form, left, right):
    return jnp.einsum(form, left, right, preferred_element_type=jnp.float32)


def matmul(left, right):
    return jnp.dot(left, right, preferred_element_type=jnp.float32)


def inner(left, right):
    return lax.dot_general(
        left, right, (((0,), (0,)), ((), ())), preferred_element_type=jnp.float32
    )


def outer_t(left, right):
    return lax.dot_general(
        left, right, (((1,), (1,)), ((), ())), preferred_element_type=jnp.float32
    )


def split_attention(flat):
    kv_width = KV_HEADS * HEAD_DIM
    edge_one = D * D
    edge_two = edge_one + D * kv_width
    edge_three = edge_two + D * kv_width
    return (
        flat[:edge_one].reshape(D, D),
        flat[edge_one:edge_two].reshape(D, kv_width),
        flat[edge_two:edge_three].reshape(D, kv_width),
        flat[edge_three:].reshape(D, D),
    )


def split_mlp(flat):
    edge_one = D * FF
    return (
        flat[:edge_one].reshape(D, FF),
        flat[edge_one : 2 * edge_one].reshape(D, FF),
        flat[2 * edge_one :].reshape(FF, D),
    )


def rope_tables():
    position = jnp.arange(SEQ_LEN).astype(jnp.float32)
    frequency = THETA ** (-(jnp.arange(HEAD_DIM // 2).astype(jnp.float32) * 2.0 / HEAD_DIM))
    angles = position[:, None] * frequency[None, :]
    return (jnp.cos(angles), jnp.sin(angles))


def rotate(tensor, cosine, sine_tab):
    half_dim = tensor.shape[-1] // 2
    lower_half = tensor[..., :half_dim]
    upper_half = tensor[..., half_dim:]
    cos_wide = cosine[None, :, None, :]
    sin_wide = sine_tab[None, :, None, :]
    return jnp.concatenate(
        [
            lower_half * cos_wide - upper_half * sin_wide,
            upper_half * cos_wide + lower_half * sin_wide,
        ],
        axis=-1,
    )


def norm_forward(stream, gain_row):
    inv_rms = lax.rsqrt(jnp.mean(stream * stream, axis=-1, keepdims=True) + EPS)
    normed = stream * inv_rms
    return (normed, inv_rms, (normed * gain_row).astype(jnp.bfloat16))


def norm_backward(grad_in, normed, inv_rms, gain_row):
    scaled = grad_in * gain_row
    grad_stream = inv_rms * (scaled - normed * jnp.mean(scaled * normed, axis=-1, keepdims=True))
    return (grad_stream, jnp.sum(grad_in * normed, axis=0))


def scores_of(queries, key_rot):
    raw_scores = mix("sqkgd,stkd->skgqt", queries, key_rot) * HEAD_DIM ** (-0.5)
    causal = jnp.arange(SEQ_LEN)[:, None] >= jnp.arange(SEQ_LEN)[None, :]
    return jnp.where(causal, raw_scores, -jnp.inf)


def forward(stream, attn_weights, mlp_weights, gain_rows):
    w_query, w_key, w_value, w_out = attn_weights
    w_gate, w_up, w_down = mlp_weights
    row_count = stream.shape[0]
    seq_count = row_count // SEQ_LEN
    group_size = HEADS // KV_HEADS
    cosine, sine_tab = rope_tables()
    normed_one, inv_one, entry_one = norm_forward(stream, gain_rows[0])
    queries = matmul(entry_one, w_query).reshape(seq_count, SEQ_LEN, HEADS, HEAD_DIM)
    queries = (
        rotate(queries, cosine, sine_tab)
        .astype(jnp.bfloat16)
        .reshape(seq_count, SEQ_LEN, KV_HEADS, group_size, HEAD_DIM)
    )
    key_rot = rotate(
        matmul(entry_one, w_key).reshape(seq_count, SEQ_LEN, KV_HEADS, HEAD_DIM), cosine, sine_tab
    ).astype(jnp.bfloat16)
    values = (
        matmul(entry_one, w_value)
        .astype(jnp.bfloat16)
        .reshape(seq_count, SEQ_LEN, KV_HEADS, HEAD_DIM)
    )
    scores = scores_of(queries, key_rot)
    row_top = jnp.max(scores, axis=-1, keepdims=True)
    log_total = row_top + jnp.log(jnp.sum(jnp.exp(scores - row_top), axis=-1, keepdims=True))
    attn_probs = jnp.exp(scores - log_total).astype(jnp.bfloat16)
    context = (
        mix("skgqt,stkd->sqkgd", attn_probs, values).astype(jnp.bfloat16).reshape(row_count, D)
    )
    middle = stream + matmul(context, w_out)
    normed_two, inv_two, entry_two = norm_forward(middle, gain_rows[1])
    gate_pre = matmul(entry_two, w_gate)
    upward = matmul(entry_two, w_up)
    hidden = (jax.nn.silu(gate_pre) * upward).astype(jnp.bfloat16)
    output = middle + matmul(hidden, w_down)
    kept_state = (
        normed_one,
        inv_one,
        entry_one,
        queries,
        key_rot,
        values,
        log_total,
        context,
        normed_two,
        inv_two,
        entry_two,
        gate_pre,
        upward,
        hidden,
    )
    return (output, kept_state)


def mlp_backward(grad_out, kept_state, mlp_weights, gain_rows):
    normed_two, inv_two, entry_two, gate_pre, upward, hidden = kept_state[8:]
    w_gate, w_up, w_down = mlp_weights
    grad_bf = grad_out.astype(jnp.bfloat16)
    grad_down = inner(hidden, grad_bf)
    grad_hidden = outer_t(grad_bf, w_down)
    sigma = jax.nn.sigmoid(gate_pre)
    grad_gate = (grad_hidden * upward * sigma * (1.0 + gate_pre * (1.0 - sigma))).astype(
        jnp.bfloat16
    )
    grad_upward = (grad_hidden * gate_pre * sigma).astype(jnp.bfloat16)
    grad_gate_w = inner(entry_two, grad_gate)
    grad_up_w = inner(entry_two, grad_upward)
    grad_entry = outer_t(grad_gate, w_gate) + outer_t(grad_upward, w_up)
    grad_norm, gain_two = norm_backward(grad_entry, normed_two, inv_two, gain_rows[1])
    flat_grad = jnp.concatenate([grad_gate_w.ravel(), grad_up_w.ravel(), grad_down.ravel()])
    return (grad_out + grad_norm, flat_grad, gain_two)


def attn_backward(grad_middle, kept_state, attn_weights, gain_rows):
    normed_one, inv_one, entry_one, queries, key_rot, values, log_total, context = kept_state[:8]
    w_query, w_key, w_value, w_out = attn_weights
    row_count = grad_middle.shape[0]
    seq_count = row_count // SEQ_LEN
    group_size = HEADS // KV_HEADS
    kv_width = KV_HEADS * HEAD_DIM
    cosine, sine_tab = rope_tables()
    grad_bf = grad_middle.astype(jnp.bfloat16)
    grad_out_w = inner(context, grad_bf)
    grad_context = (
        outer_t(grad_bf, w_out)
        .astype(jnp.bfloat16)
        .reshape(seq_count, SEQ_LEN, KV_HEADS, group_size, HEAD_DIM)
    )
    soft_probs = jnp.exp(scores_of(queries, key_rot) - log_total)
    grad_soft = mix("sqkgd,stkd->skgqt", grad_context, values)
    row_dot = jnp.sum(soft_probs * grad_soft, axis=-1, keepdims=True)
    grad_scores = (soft_probs * (grad_soft - row_dot) * HEAD_DIM ** (-0.5)).astype(jnp.bfloat16)
    grad_query = mix("skgqt,stkd->sqkgd", grad_scores, key_rot).reshape(
        seq_count, SEQ_LEN, HEADS, HEAD_DIM
    )
    grad_query = rotate(grad_query, cosine, -sine_tab).astype(jnp.bfloat16).reshape(row_count, D)
    grad_key = (
        rotate(mix("skgqt,sqkgd->stkd", grad_scores, queries), cosine, -sine_tab)
        .astype(jnp.bfloat16)
        .reshape(row_count, kv_width)
    )
    grad_value = (
        mix("skgqt,sqkgd->stkd", soft_probs.astype(jnp.bfloat16), grad_context)
        .astype(jnp.bfloat16)
        .reshape(row_count, kv_width)
    )
    grad_entry = (
        outer_t(grad_query, w_query) + outer_t(grad_key, w_key) + outer_t(grad_value, w_value)
    )
    grad_norm, gain_one = norm_backward(grad_entry, normed_one, inv_one, gain_rows[0])
    flat_grad = jnp.concatenate(
        [
            inner(entry_one, grad_query).ravel(),
            inner(entry_one, grad_key).ravel(),
            inner(entry_one, grad_value).ravel(),
            grad_out_w.ravel(),
        ]
    )
    return (grad_middle + grad_norm, flat_grad, gain_one)


def reduce_mlp(mlp_flat):
    devices = lax.axis_size("dp")
    grid = mlp_flat.reshape(devices, -1)
    third = grid.shape[1] // 3
    pieces = []
    for index in range(3):
        columns = grid[:, index * third : (index + 1) * third]
        pieces.append(lax.psum_scatter(columns, "dp", scatter_dimension=0, tiled=True))
    return jnp.concatenate(pieces, axis=1).reshape(-1)


def reduce_attn(attn_flat):
    devices = lax.axis_size("dp")
    grid = attn_flat.reshape(devices, -1)
    return lax.psum_scatter(grid, "dp", scatter_dimension=0, tiled=True).reshape(-1)


def body(inputs, cotangent, attn_shard, mlp_shard, gain_rows):
    attn_full, mlp_full = (
        lax.all_gather(attn_shard, "dp", axis=0, tiled=True),
        lax.all_gather(mlp_shard, "dp", axis=0, tiled=True),
    )
    outputs, kept_state = forward(
        inputs, split_attention(attn_full), split_mlp(mlp_full), gain_rows
    )
    attn_again, mlp_again, outputs = lax.optimization_barrier((attn_shard, mlp_shard, outputs))
    attn_back, mlp_back = (
        lax.all_gather(attn_again, "dp", axis=0, tiled=True),
        lax.all_gather(mlp_again, "dp", axis=0, tiled=True),
    )
    attn_weights = split_attention(attn_back)
    grad_middle, mlp_flat, gain_two = mlp_backward(
        cotangent, kept_state, split_mlp(mlp_back), gain_rows
    )
    grad_input, attn_flat, gain_one = attn_backward(
        grad_middle, kept_state, attn_weights, gain_rows
    )
    attn_grad = reduce_attn(attn_flat)
    mlp_grad = reduce_mlp(mlp_flat)
    gain_grad = lax.psum(jnp.stack([gain_one, gain_two]), "dp")
    return (outputs, grad_input, attn_grad, mlp_grad, gain_grad)


def solution(mesh):
    placed = (P("dp", None), P("dp", None), P("dp"), P("dp"), P())
    return jax.shard_map(
        body,
        mesh=mesh,
        in_specs=placed,
        out_specs=(P("dp", None), P("dp", None), P("dp"), P("dp"), P()),
        check_vma=False,
    )
```

profile of v0, /device:TPU:0, one launch (start us, length us, event | category | flops | bytes accessed | tf_op | source)
XLA Modules:
  0.0 639.0 jit_solution(4361602386090001413)
XLA Ops:
  7.2 0.7 all-gather.5.cloned.1.call-update
  7.9 0.7 all-gather.7.cloned.1.call-update
  8.7 0.6 iota_compare_fusion
  9.4 1.1 multiply_reduce_fusion.5
  10.5 1.4 slice_reduce_fusion
  11.9 0.8 fusion.22
  12.7 1.2 multiply_convert_fusion.4
  13.9 55.1 %all-gather.5.cloned.1.call-done = bf16[884736]{0:T(1024)(128)(2,1)} async-done(((bf16[27648]{0:T(1024)(128)(2,1)}), bf16[884736]{0:T(1024)(128)(2,1)}) %all-gather.5.cloned.1.call-update) | async-done | bytes 1769488 | tf_op jit(solution)/shard_map/all_gather | solution.py:240
  69.0 1.1 fusion.32
  70.5 1.4 fusion.31
  77.0 59.5 %all-gather.7.cloned.1.call-done = bf16[2654208]{0:T(1024)(128)(2,1)} async-done(((bf16[82944]{0:T(1024)(128)(2,1)}), bf16[2654208]{0:T(1024)(128)(2,1)}) %all-gather.7.cloned.1.call-update) | async-done | bytes 5308432 | tf_op jit(solution)/shard_map/all_gather | solution.py:241
  136.5 5.0 fusion.28
  141.6 4.3 slice.242
  145.8 4.4 slice.240
  150.2 4.5 slice.238
  154.7 2.2 fusion.34
  157.0 1.7 multiply_convert_fusion.2
  158.7 0.8 copy-done.17
  159.5 1.4 convolution_add_fusion.3
  161.7 3.8 fusion.16
  165.6 5.4 reshape.449
  170.9 44.1 %all-gather.11.cloned.1.call-done = bf16[884736]{0:T(1024)(128)(2,1)} async-done(((bf16[27648]{0:T(1024)(128)(2,1)}), bf16[884736]{0:T(1024)(128)(2,1)}) %all-gather.11.cloned.1.call-update) | async-done | bytes 1769488 | tf_op jit(solution)/shard_map/all_gather | solution.py:248
  215.0 2.4 fusion.29
  217.5 1.7 slice.250
  219.2 63.2 %all-gather.9.cloned.1.call-done = bf16[2654208]{0:T(1024)(128)(2,1)} async-done(((bf16[82944]{0:T(1024)(128)(2,1)}), bf16[2654208]{0:T(1024)(128)(2,1)}) %all-gather.9.cloned.1.call-update) | async-done | bytes 5308432 | tf_op jit(solution)/shard_map/all_gather | solution.py:249
  282.4 5.0 fusion.27
  287.4 4.4 slice.248
  291.8 4.4 slice.246
  296.3 4.3 slice.244
  300.5 3.4 multiply_convert_fusion
  304.0 0.8 fusion.35
  304.8 1.1 copy-done.8
  305.9 1.5 multiply_reduce_fusion
  307.6 1.5 fusion.13
  311.6 1.1 convolution_bitcast_fusion.4
  312.7 1.1 fusion.19
  313.8 0.7 fusion.42
  314.9 2.4 fusion.41
  317.3 1.1 fusion.40
  318.4 2.2 reshape.443
  320.6 2.9 reshape.444
  323.4 1.0 subtract_convert_fusion.2
  324.4 1.9 subtract_convert_fusion
  326.9 2.1 fusion.39
  329.0 2.1 reshape.442
  331.1 1.0 pad_maximum_fusion.4
  332.2 0.7 copy-done.12
  332.9 2.6 fusion.38
  335.4 2.8 reshape.441
  338.2 4.0 pad_maximum_fusion.1
  342.2 3.5 reshape.445
  345.7 2.0 reshape.448
  347.8 4.9 reshape.447
  352.7 10.0 %pad_maximum_fusion = f32[2654208]{0:T(1024)} fusion(f32[884736]{0:T(1024)S(1)} %copy-done, f32[884736]{0:T(1024)} %reshape.448, f32[884736]{0:T(1024)} %reshape.447), kind=kLoop, calls=%fused_computation | loop fusion | flops 5308416 | bytes 21233664 | tf_op jit(solution)/shard_map/concatenate | solution.py:169
  362.7 8.7 %reshape.450 = f32[32,82944]{1,0:T(8,128)} reshape(f32[2654208]{0:T(1024)} %pad_maximum_fusion) | data formatting | bytes 21233664 | tf_op jit(solution)/shard_map/reshape | solution.py:223
  371.4 8.2 %fusion.26 = (f32[32,27648]{1,0:T(8,128)}, f32[32,27648]{1,0:T(8,128)}, f32[32,27648]{1,0:T(8,128)}) fusion(f32[32,82944]{1,0:T(8,128)} %reshape.450), kind=kLoop, calls=%fused_computation.87 | loop fusion | bytes 21233664 | tf_op jit(solution)/shard_map/slice | solution.py:227
  379.7 1.1 fusion.30
  383.1 41.4 %psum.7 = f32[2,576]{1,0:T(2,128)} all-reduce(f32[2,576]{1,0:T(2,128)S(1)} %pad_maximum_fusion.8), channel_id=1, replica_groups=mesh['dp'=32] {'dp'}, use_global_device_ids=true, to_apply=%region_13.14 | all-reduce | flops 1152 | bytes 9216 | tf_op jit(solution)/shard_map/psum | solution.py:260
  424.6 0.9 multiply_add_fusion
  425.5 201.3 %all-reduce.7.cloned.1.call-done = (f32[32,27648]{1,0:T(8,128)}, f32[32,27648]{1,0:T(8,128)}, f32[32,27648]{1,0:T(8,128)}, f32[32,27648]{1,0:T(8,128)}) async-done(((f32[32,27648]{1,0:T(8,128)}, f32[32,27648]{1,0:T(8,128)}, f32[32,27648]{1,0:T(8,128)}, f32[32,27648]{1,0:T(8,128)}), (f32[32,27648]{1,0:T(8,128)}, f32[32,27648]{1,0:T(8,128)}, f32[32,27648]{1,0:T(8,128)}, ...) | async-done | bytes 14155792
  626.8 1.9 constant_dynamic-slice_fusion.3
  628.6 1.2 constant_dynamic-slice_fusion.2
  629.9 1.6 constant_dynamic-slice_fusion
  631.5 1.0 pad_maximum_fusion.2
  (130 shorter events, 12.1 us)
Async XLA Ops:
  7.2 61.8 %all-gather.5.cloned.1.call-start = ((), (), s32[]{:S(2)}) async-start(), calls=%async_computation | async-start | bytes 1824768 | tf_op jit(solution)/shard_map/all_gather | solution.py:240
  7.9 128.6 %all-gather.7.cloned.1.call-start = ((), (), s32[]{:S(2)}) async-start(), calls=%async_computation.1 | async-start | bytes 5474304 | tf_op jit(solution)/shard_map/all_gather | solution.py:241
  8.6 206.4 %all-gather.11.cloned.1.call-start = ((), (), s32[]{:S(2)}) async-start(), calls=%async_computation.3 | async-start | bytes 1824768 | tf_op jit(solution)/shard_map/all_gather | solution.py:248
  10.5 61.3 %copy-start.38 = (f32[192]{0:T(256)}, f32[192]{0:T(256)S(1)}, u32[]{:S(2)}) copy-start(f32[192]{0:T(256)S(1)} %add_rsqrt_fusion.1) | copy-start | bytes 2308
  12.7 61.6 %copy-start.28 = (f32[192,32]{0,1:T(8,128)}, f32[192,32]{0,1:T(8,128)S(1)}, u32[]{:S(2)}) copy-start(f32[192,32]{0,1:T(8,128)S(1)} %get-tuple-element.50) | copy-start | bytes 73732
  13.9 61.4 %copy-start.3 = (bf16[192,576]{1,0:T(8,128)(2,1)}, bf16[192,576]{1,0:T(8,128)(2,1)S(1)}, u32[]{:S(2)}) copy-start(bf16[192,576]{1,0:T(8,128)(2,1)S(1)} %multiply_convert_fusion.4) | copy-start | bytes 663556
  73.6 0.9 copy-start.37
  74.3 0.9 copy-start.31
  74.4 0.9 copy-start.33
  74.5 0.8 copy-start.29
  75.3 1.0 copy-start.1
  75.7 1.2 copy-start.35
  76.8 64.7 %copy-start.40 = (f32[192]{0:T(256)}, f32[192]{0:T(256)S(1)}, u32[]{:S(2)}) copy-start(f32[192]{0:T(256)S(1)} %add_rsqrt_fusion) | copy-start | bytes 2308
  77.0 80.0 %copy-start.10 = (bf16[192,576]{1,0:T(8,128)(2,1)}, bf16[192,576]{1,0:T(8,128)(2,1)S(1)}, u32[]{:S(2)}) copy-start(bf16[192,576]{1,0:T(8,128)(2,1)S(1)} %multiply_convert_fusion.3) | copy-start | bytes 663556
  154.7 2.2 copy-start.22
  157.0 1.7 copy-start.23
  157.0 2.5 copy-start.5
  158.7 0.8 copy-start.17
  159.5 2.3 copy-start.20
  160.9 121.5 %all-gather.9.cloned.1.call-start = ((), (), s32[]{:S(2)}) async-start(), calls=%async_computation.2 | async-start | bytes 5474304 | tf_op jit(solution)/shard_map/all_gather | solution.py:249
  161.5 465.3 %all-reduce.7.cloned.1.call-start = ((), (), s32[]{:S(2)}) async-start(), calls=%async_computation.4 | async-start | bytes 28311552
  300.5 3.5 copy-start.9
  304.0 3.4 copy-start.15
  304.0 3.4 copy-start.18
  304.0 1.9 copy-start.8
  304.0 1.9 copy-start.36
  304.0 1.9 copy-start.41
  305.9 1.5 copy-start.21
  307.6 1.5 copy-start.6
  310.1 7.1 %copy-start.24 = (bf16[3,64,192]{2,1,0:T(8,128)(2,1)}, bf16[3,64,192]{2,1,0:T(8,128)(2,1)S(1)}, u32[]{:S(2)}) copy-start(bf16[3,64,192]{2,1,0:T(8,128)(2,1)S(1)} %fusion.6) | copy-start | bytes 221188
  310.7 0.9 copy-start.30
  310.7 2.0 copy-start.32
  310.7 2.0 copy-start.34
  311.6 2.2 copy-start.11
  311.6 2.2 copy-start.16
  313.8 1.1 copy-start.19
  314.9 2.4 copy-start.4
  326.3 0.6 copy-start.26
  332.2 0.7 copy-start.12
  347.8 4.9 copy-start
  379.6 1.4 copy-start.14
  379.6 2.2 copy-start.42
  379.6 2.2 copy-start.25
  380.8 1.4 copy-start.27
  381.0 1.5 copy-start.2
  381.0 1.4 copy-start.13
  381.1 1.4 copy-start.39
  382.2 42.4 %copy-start.7 = (f32[192,576]{1,0:T(8,128)S(1)}, f32[192,576]{1,0:T(8,128)}, u32[]{:S(2)}) copy-start(f32[192,576]{1,0:T(8,128)} %copy-done.6) | copy-start | bytes 1327108
Sparse Core Ops, SparseCore 0:
  10.8 58.1 all-gather.4
  71.9 64.5 all-gather.6
  161.0 53.9 all-gather.10
  217.8 64.5 all-gather.8
  379.7 246.9 all-reduce.6
where the time goes:
time: 640 us; the launch traced here: 639 us
  waiting for transfers between devices  425 us (66%)
  local copies, waits for them, and re-layouts  100 us (16%)
  blocking collectives  41.4 us (6%)
  matrix products  32.3 us (5%)
  other arithmetic  24.8 us (4%)
  between operations  14.5 us (2%)
    unnamed x6, waiting for transfers between devices  203 us
    all_gather x1, waiting for transfers between devices, body(): lax.all_gather(mlp_again, 'dp', axis=0, tiled=True)  63.2 us
    all_gather x1, waiting for transfers between devices, body(): lax.all_gather(mlp_shard, 'dp', axis=0, tiled=True)  59.5 us
    all_gather x1, waiting for transfers between devices, body(): lax.all_gather(attn_shard, 'dp', axis=0, tiled=True)  55.1 us
    all_gather x1, waiting for transfers between devices, body(): lax.all_gather(attn_again, 'dp', axis=0, tiled=True)  44.1 us
    psum x1, blocking collectives, body(): gain_grad = lax.psum(jnp.stack([gain_one, gain_two]), 'dp')  41.4 us
    dot_general x7, matrix products, inner(): lax.dot_general(left, right, (((0,), (0,)), ((), ())), preferred_element_...  14.2 us
    slice x3, local copies, waits for them, and re-layouts, split_mlp(): flat[edge_one:2 * edge_one].reshape(D, FF)  13.8 us
  transfers between devices with their start and end apart: 5, of which 5 were waited for; matrix products, arithmetic and copies ran while one was open for 5% of the time, Pallas kernels for 0%

commit v1 on v0

--- a/solution.py
+++ b/solution.py
@@ -1,7 +1,13 @@
 import jax
 import jax.numpy as jnp
 from jax import lax
+from jax.experimental import pallas as pl
+from jax.experimental.pallas import tpu as pltpu
 from jax.sharding import PartitionSpec as P
+
+LANES = 128
+PIECES = 6
+MESH = pl.DeviceIdType.MESH
 
 D = 576
 HEADS = 9
@@ -151,6 +157,10 @@
     return (output, kept_state)
 
 
+def flatten(grads):
+    return jnp.concatenate([grad.astype(jnp.bfloat16).ravel() for grad in grads])
+
+
 def mlp_backward(grad_out, kept_state, mlp_weights, gain_rows):
     normed_two, inv_two, entry_two, gate_pre, upward, hidden = kept_state[8:]
     w_gate, w_up, w_down = mlp_weights
@@ -166,7 +176,7 @@
     grad_up_w = inner(entry_two, grad_upward)
     grad_entry = outer_t(grad_gate, w_gate) + outer_t(grad_upward, w_up)
     grad_norm, gain_two = norm_backward(grad_entry, normed_two, inv_two, gain_rows[1])
-    flat_grad = jnp.concatenate([grad_gate_w.ravel(), grad_up_w.ravel(), grad_down.ravel()])
+    flat_grad = flatten([grad_gate_w, grad_up_w, grad_down])
     return (grad_out + grad_norm, flat_grad, gain_two)
 
 
@@ -207,57 +217,256 @@
         outer_t(grad_query, w_query) + outer_t(grad_key, w_key) + outer_t(grad_value, w_value)
     )
     grad_norm, gain_one = norm_backward(grad_entry, normed_one, inv_one, gain_rows[0])
-    flat_grad = jnp.concatenate(
+    flat_grad = flatten(
         [
-            inner(entry_one, grad_query).ravel(),
-            inner(entry_one, grad_key).ravel(),
-            inner(entry_one, grad_value).ravel(),
-            grad_out_w.ravel(),
+            inner(entry_one, grad_query),
+            inner(entry_one, grad_key),
+            inner(entry_one, grad_value),
+            grad_out_w,
         ]
     )
     return (grad_middle + grad_norm, flat_grad, gain_one)
 
 
-def reduce_mlp(mlp_flat):
+def bit_count(devices):
+    bits = devices.bit_length() - 1
+    assert 1 << bits == devices
+    return bits
+
+
+def bit_orders(bits):
+    plain = list(range(bits - 1, -1, -1))
+    swapped = list(plain)
+    if bits > 2:
+        first, second = swapped.index(2), swapped.index(1)
+        swapped[first], swapped[second] = swapped[second], swapped[first]
+    return [plain if piece % 2 == 0 else swapped for piece in range(PIECES)]
+
+
+def coordinates(bits):
+    me = lax.axis_index("dp")
+    digits = [lax.rem(me // (1 << bit), 2) for bit in range(bits)]
+    partners = [me + (1 << bit) * (1 - 2 * digits[bit]) for bit in range(bits)]
+    return digits, partners
+
+
+def meet(partners):
+    barrier = pltpu.get_barrier_semaphore()
+    for partner in partners:
+        pl.semaphore_signal(barrier, inc=1, device_id=(partner,), device_id_type=MESH)
+    pl.semaphore_wait(barrier, len(partners))
+
+
+def pick(bits, fixed):
+    return tuple(fixed.get(bit, slice(None)) for bit in range(bits - 1, -1, -1))
+
+
+def gather_kernel(bits, shard_ref, full_ref, local_sem, send_sem, recv_sem):
+    digits, partners = coordinates(bits)
+    orders = bit_orders(bits)
+    own = pltpu.make_async_copy(
+        shard_ref, full_ref.at[pick(bits, dict(enumerate(digits)))], local_sem
+    )
+    own.start()
+    meet(partners)
+    own.wait()
+    flights = {}
+    for stage in range(bits):
+        for piece in range(PIECES):
+            if stage > 0:
+                flights[piece, stage - 1].wait_recv()
+            order = orders[piece]
+            fixed = {bit: digits[bit] for bit in order[stage:]}
+            block = full_ref.at[pick(bits, fixed) + (piece,)]
+            copy = pltpu.make_async_remote_copy(
+                src_ref=block,
+                dst_ref=block,
+                send_sem=send_sem.at[piece, stage],
+                recv_sem=recv_sem.at[piece, stage],
+                device_id=(partners[order[stage]],),
+                device_id_type=MESH,
+            )
+            copy.start()
+            flights[piece, stage] = copy
+    for piece in range(PIECES):
+        flights[piece, bits - 1].wait_recv()
+    for copy in flights.values():
+        copy.wait_send()
+
+
+def gather(shard):
     devices = lax.axis_size("dp")
-    grid = mlp_flat.reshape(devices, -1)
-    third = grid.shape[1] // 3
-    pieces = []
-    for index in range(3):
-        columns = grid[:, index * third : (index + 1) * third]
-        pieces.append(lax.psum_scatter(columns, "dp", scatter_dimension=0, tiled=True))
-    return jnp.concatenate(pieces, axis=1).reshape(-1)
-
-
-def reduce_attn(attn_flat):
+    bits = bit_count(devices)
+    rows = shard.shape[0] // PIECES
+    full = pl.pallas_call(
+        lambda *refs: gather_kernel(bits, *refs),
+        out_shape=jax.ShapeDtypeStruct((2,) * bits + (PIECES, rows, LANES), shard.dtype),
+        in_specs=[pl.BlockSpec(memory_space=pltpu.VMEM)],
+        out_specs=pl.BlockSpec(memory_space=pltpu.VMEM),
+        scratch_shapes=[
+            pltpu.SemaphoreType.DMA,
+            pltpu.SemaphoreType.DMA((PIECES, bits)),
+            pltpu.SemaphoreType.DMA((PIECES, bits)),
+        ],
+        compiler_params=pltpu.CompilerParams(
+            collective_id=0, has_side_effects=True, vmem_limit_bytes=60 << 20
+        ),
+    )(shard.reshape(PIECES, rows, LANES))
+    return full.reshape(devices, PIECES * rows, LANES)
+
+
+def scatter_kernel(bits, total_ref, gain_ref, out_ref, gain_out, *scratch):
+    landing = scratch[:bits]
+    held = scratch[bits : 2 * bits - 1]
+    gain_sent, gain_landing = scratch[2 * bits - 1 : 2 * bits + 1]
+    send_sem, recv_sem, gain_send, gain_recv = scratch[2 * bits + 1 :]
+    digits, partners = coordinates(bits)
+    orders = [order[::-1] for order in bit_orders(bits)]
+    meet(partners)
+    flights = {}
+    gain_flights = {}
+
+    def block_index(order, stage, digit):
+        if stage == 0:
+            return pick(bits, {order[0]: digit})
+        left = [bit for bit in range(bits - 1, -1, -1) if bit not in order[:stage]]
+        return tuple(digit if bit == order[stage] else slice(None) for bit in left)
+
+    def source(piece, stage):
+        return total_ref if stage == 0 else held[stage - 1]
+
+    def launch(piece, stage):
+        order = orders[piece]
+        bit = order[stage]
+        lead = block_index(order, stage, 1 - digits[bit])
+        if stage == 0:
+            src = total_ref.at[lead + (piece,)]
+        else:
+            src = held[stage - 1].at[(piece,) + lead]
+        copy = pltpu.make_async_remote_copy(
+            src_ref=src,
+            dst_ref=landing[stage].at[piece],
+            send_sem=send_sem.at[piece, stage],
+            recv_sem=recv_sem.at[piece, stage],
+            device_id=(partners[bit],),
+            device_id_type=MESH,
+        )
+        copy.start()
+        flights[piece, stage] = copy
+
+    def absorb(piece, stage):
+        flights[piece, stage].wait_recv()
+        order = orders[piece]
+        bit = order[stage]
+        lead = block_index(order, stage, digits[bit])
+        free = len(lead) - 1
+        for number in range(1 << free):
+            picks = [(number >> place) & 1 for place in range(free - 1, -1, -1)]
+            spot = iter(picks)
+            where = tuple(next(spot) if isinstance(item, slice) else item for item in lead)
+            if stage == 0:
+                mine = total_ref[where + (piece,)]
+            else:
+                mine = held[stage - 1][(piece,) + where]
+            other = landing[stage][(piece,) + tuple(picks)]
+            value = mine.astype(jnp.float32) + other.astype(jnp.float32)
+            if stage == bits - 1:
+                out_ref[piece] = value
+            else:
+                held[stage][(piece,) + tuple(picks)] = value.astype(jnp.bfloat16)
+
+    def launch_gain(stage):
+        copy = pltpu.make_async_remote_copy(
+            src_ref=gain_ref if stage == 0 else gain_sent.at[stage],
+            dst_ref=gain_landing.at[stage],
+            send_sem=gain_send.at[stage],
+            recv_sem=gain_recv.at[stage],
+            device_id=(partners[stage],),
+            device_id_type=MESH,
+        )
+        copy.start()
+        gain_flights[stage] = copy
+
+    def absorb_gain(stage):
+        gain_flights[stage].wait_recv()
+        mine = gain_ref[...] if stage == 0 else gain_sent[stage]
+        value = mine + gain_landing[stage]
+        if stage == bits - 1:
+            gain_out[...] = value
+        else:
+            gain_sent[stage + 1] = value
+
+    for stage in range(bits):
+        if stage > 0:
+            absorb_gain(stage - 1)
+        launch_gain(stage)
+        for piece in range(PIECES):
+            if stage > 0:
+                absorb(piece, stage - 1)
+            launch(piece, stage)
+    absorb_gain(bits - 1)
+    for piece in range(PIECES):
+        absorb(piece, bits - 1)
+    for copy in list(flights.values()) + list(gain_flights.values()):
+        copy.wait_send()
+
+
+def scatter(total, gains):
     devices = lax.axis_size("dp")
-    grid = attn_flat.reshape(devices, -1)
-    return lax.psum_scatter(grid, "dp", scatter_dimension=0, tiled=True).reshape(-1)
+    bits = bit_count(devices)
+    rows = total.shape[1] // PIECES
+    slots = [(PIECES,) + (2,) * (bits - 1 - stage) + (rows, LANES) for stage in range(bits)]
+    vmem = pl.BlockSpec(memory_space=pltpu.VMEM)
+    out, gain_sum = pl.pallas_call(
+        lambda *refs: scatter_kernel(bits, *refs),
+        out_shape=(
+            jax.ShapeDtypeStruct((PIECES, rows, LANES), jnp.float32),
+            jax.ShapeDtypeStruct(gains.shape, jnp.float32),
+        ),
+        in_specs=[vmem, vmem],
+        out_specs=(vmem, vmem),
+        scratch_shapes=[pltpu.VMEM(slot, jnp.bfloat16) for slot in slots]
+        + [pltpu.VMEM(slot, jnp.bfloat16) for slot in slots[:-1]]
+        + [
+            pltpu.VMEM((bits,) + gains.shape, jnp.float32),
+            pltpu.VMEM((bits,) + gains.shape, jnp.float32),
+            pltpu.SemaphoreType.DMA((PIECES, bits)),
+            pltpu.SemaphoreType.DMA((PIECES, bits)),
+            pltpu.SemaphoreType.DMA((bits,)),
+            pltpu.SemaphoreType.DMA((bits,)),
+        ],
+        compiler_params=pltpu.CompilerParams(
+            collective_id=1, has_side_effects=True, vmem_limit_bytes=60 << 20
+        ),
+    )(total.reshape((2,) * bits + (PIECES, rows, LANES)), gains)
+    return out.reshape(PIECES * rows, LANES), gain_sum
 
 
 def body(inputs, cotangent, attn_shard, mlp_shard, gain_rows):
-    attn_full, mlp_full = (
-        lax.all_gather(attn_shard, "dp", axis=0, tiled=True),
-        lax.all_gather(mlp_shard, "dp", axis=0, tiled=True),
-    )
-    outputs, kept_state = forward(
-        inputs, split_attention(attn_full), split_mlp(mlp_full), gain_rows
-    )
-    attn_again, mlp_again, outputs = lax.optimization_barrier((attn_shard, mlp_shard, outputs))
-    attn_back, mlp_back = (
-        lax.all_gather(attn_again, "dp", axis=0, tiled=True),
-        lax.all_gather(mlp_again, "dp", axis=0, tiled=True),
-    )
-    attn_weights = split_attention(attn_back)
-    grad_middle, mlp_flat, gain_two = mlp_backward(
-        cotangent, kept_state, split_mlp(mlp_back), gain_rows
-    )
+    devices = lax.axis_size("dp")
+    attn_rows = attn_shard.shape[0] // LANES
+    packed = jnp.concatenate(
+        [attn_shard.reshape(-1, LANES), mlp_shard.reshape(-1, LANES)], axis=0
+    )
+    full = gather(packed)
+    attn_weights = split_attention(full[:, :attn_rows].reshape(-1))
+    mlp_weights = split_mlp(full[:, attn_rows:].reshape(-1))
+    outputs, kept_state = forward(inputs, attn_weights, mlp_weights, gain_rows)
+    grad_middle, mlp_flat, gain_two = mlp_backward(cotangent, kept_state, mlp_weights, gain_rows)
     grad_input, attn_flat, gain_one = attn_backward(
         grad_middle, kept_state, attn_weights, gain_rows
     )
-    attn_grad = reduce_attn(attn_flat)
-    mlp_grad = reduce_mlp(mlp_flat)
-    gain_grad = lax.psum(jnp.stack([gain_one, gain_two]), "dp")
+    total = jnp.concatenate(
+        [
+            attn_flat.reshape(devices, -1, LANES),
+            mlp_flat.reshape(devices, -1, LANES),
+        ],
+        axis=1,
+    )
+    gains = jnp.stack([gain_one, gain_two])
+    summed, gain_grad = scatter(total, gains)
+    attn_grad = summed[:attn_rows].reshape(-1)
+    mlp_grad = summed[attn_rows:].reshape(-1)
     return (outputs, grad_input, attn_grad, mlp_grad, gain_grad)
 
 

time: 640 us -> 230 us (0.36)
  waiting for transfers between devices: 425 us -> 0 us
  Pallas kernels: 0 us -> 105 us
  blocking collectives: 41.4 us -> 0 us
  local copies, waits for them, and re-layouts: 100 us -> 66.9 us
  between operations: 14.5 us -> 1.26 us
    all_gather x4 -> x0, waiting for transfers between devices: 222 us -> none  [the longest x1 63.2 us: body(): lax.all_gather(mlp_again, 'dp', axis=0, tiled=True)]
    unnamed x6 -> x0, waiting for transfers between devices: 203 us -> none
    pallas_call x0 -> x2, Pallas kernels: none -> 105 us  [the longest x1 53.3 us: gather(): pl.pallas_call(lambda *refs: gather_kernel(bits, *refs), out_shape=jax.Sh...]
    psum x1 -> x0, blocking collectives: 41.4 us -> none  [body(): gain_grad = lax.psum(jnp.stack([gain_one, gain_two]), 'dp')]
    slice x9 -> x1, local copies, waits for them, and re-layouts: 26 us -> 5.16 us  [body(): mlp_weights = split_mlp(full[:, attn_rows:].reshape(-1))]
    reshape x9 -> x14, local copies, waits for them, and re-layouts: 34.5 us -> 24.3 us  [the longest x7 19.2 us: flatten(): grad.astype(jnp.bfloat16).ravel()]
    slice x3 -> x1, local copies, waits for them, and re-layouts: 13.6 us -> 10.7 us  [split_mlp(): flat[2 * edge_one:].reshape(FF, D)]
    concatenate x3 -> x4, other arithmetic: 15 us -> 16 us  [the longest x2 8.48 us: flatten(): jnp.concatenate([grad.astype(jnp.bfloat16).ravel() for grad in grads])]
  transfers between devices with their start and end apart: 5 -> 0, of which waited for: 5 -> 0; matrix products, arithmetic and copies ran while one was open for 5% -> 0% of each run, Pallas kernels for 0% -> 0%
where the time goes in v1:
time: 230 us; the launch traced here: 228 us
  Pallas kernels  105 us (46%)
  local copies, waits for them, and re-layouts  66.9 us (29%)
  matrix products  31.7 us (14%)
  other arithmetic  23.3 us (10%)
    pallas_call x1, Pallas kernels, gather(): pl.pallas_call(lambda *refs: gather_kernel(bits, *refs), out_shape=jax.Sh...  53.3 us
    pallas_call x1, Pallas kernels, scatter(): pl.pallas_call(lambda *refs: scatter_kernel(bits, *refs), out_shape=(jax....  51.3 us
    reshape x7, local copies, waits for them, and re-layouts, flatten(): grad.astype(jnp.bfloat16).ravel()  19.2 us
    dot_general x7, matrix products, inner(): lax.dot_general(left, right, (((0,), (0,)), ((), ())), preferred_element_...  12.7 us
    slice x1, local copies, waits for them, and re-layouts, split_mlp(): flat[2 * edge_one:].reshape(FF, D)  10.7 us
    slice x1, local copies, waits for them, and re-layouts, split_mlp(): flat[:edge_one].reshape(D, FF)  10.7 us
    concatenate x2, other arithmetic, flatten(): jnp.concatenate([grad.astype(jnp.bfloat16).ravel() for grad in grads])  8.48 us
    dot_general x7, matrix products, matmul(): return jnp.dot(left, right, preferred_element_type=jnp.float32)  8.22 us

profile of v1, /device:TPU:0, one launch (start us, length us, event | category | flops | bytes accessed | tf_op | source)
XLA Modules:
  0.0 227.8 jit_solution(6467964139656162034)
XLA Ops:
  0.6 1.1 multiply_reduce_fusion.5
  1.8 0.8 slice_reduce_fusion
  2.6 0.6 iota_compare_fusion
  3.3 0.8 fusion.37
  4.1 1.6 pad_maximum_fusion.4
  5.7 1.1 multiply_convert_fusion.4
  6.8 53.3 %shard_map.92 = bf16[2,2,2,2,2,6,144,128]{7,6,5,4,3,2,1,0:T(8,128)(2,1)} custom-call(bf16[6,144,128]{2,1,0:T(8,128)(2,1)} %bitcast.159), custom_call_target="tpu_custom_call" | custom-call | tf_op jit(solution)/shard_map/pallas_call | solution.py:301
  60.1 1.1 fusion.42
  61.9 0.7 fusion.35
  62.8 0.3 convolution_convert_fusion.9
  63.1 1.4 fusion.41
  64.6 5.2 %slice.108 = bf16[32,648,128]{2,1,0:T(8,128)(2,1)} slice(bf16[32,864,128]{2,1,0:T(8,128)(2,1)} %bitcast.140), slice={[0:32], [216:864], [0:128]} | slice | bytes 10616832 | tf_op jit(solution)/shard_map/slice | solution.py:453
  69.7 0.6 reshape.423
  70.3 0.6 reshape.420
  70.9 0.4 copy.19
  71.3 0.4 convolution_bitcast_fusion.1
  72.1 0.5 fusion.43
  72.6 0.3 exponential_reduce_fusion
  73.0 0.4 convolution_convert_fusion.5
  73.4 0.3 copy-done
  73.6 0.5 multiply_reduce_fusion.4
  74.2 0.8 copy-done.7
  75.1 10.7 %slice.89 = bf16[1728,1536]{1,0:T(8,128)(2,1)} reshape(bf16[32,648,128]{2,1,0:T(8,128)(2,1)} %slice.108) | data formatting | bytes 10616832 | tf_op jit(solution)/shard_map/slice | solution.py:60
  85.8 10.7 %slice.92 = bf16[4608,576]{1,0:T(8,128)(2,1)} reshape(bf16[32,648,128]{2,1,0:T(8,128)(2,1)} %slice.108) | data formatting | bytes 10616832 | tf_op jit(solution)/shard_map/slice | solution.py:62
  96.5 2.5 %convolution_bitcast_fusion = f32[192,1536]{1,0:T(8,128)S(1)} fusion(bf16[4608,576]{1,0:T(8,128)(2,1)} %slice.92, f32[192,576]{1,0:T(8,128)S(1)} %copy-done.6), kind=kOutput, calls=%fused_computation.5 | convolution fusion | flops 339849216 | bytes 3588096 | tf_op jit(solution)/shard_map/dot_general | solution.py:39
  99.0 2.1 fusion.9
  101.1 1.0 multiply_convert_fusion.1
  102.2 3.6 %fusion.20 = f32[192,576]{1,0:T(8,128)} fusion(f32[192,576]{1,0:T(8,128)S(1)} %copy-done.8, bf16[192,1536]{1,0:T(8,128)(2,1)S(1)} %get-tuple-element.20, bf16[4608,576]{1,0:T(8,128)(2,1)} %slice.92), kind=kOutput, calls=%fused_computation.35 | convolution fusion | flops 339849216 | bytes 3440640 | tf_op jit(solution)/shard_map/dot_general | solution.py:29
  105.8 0.8 fusion.7
  106.6 0.9 multiply_reduce_fusion
  107.8 0.9 copy-done.5
  108.7 1.1 convolution_convert_fusion.8
  109.8 1.8 copy.21
  111.6 1.4 fusion.23
  113.0 1.1 fusion.45
  114.1 0.9 convolution_convert_fusion.6
  115.0 1.8 copy.26
  116.8 2.0 reshape.430
  118.8 2.2 convolution_convert_fusion.3
  121.1 2.6 %reshape.431 = bf16[331776]{0:T(1024)(128)(2,1)} reshape(bf16[576,576]{1,0:T(8,128)(2,1)} %convolution_convert_fusion.3) | data formatting | bytes 1327104 | tf_op jit(solution)/shard_map/reshape | solution.py:161
  123.6 2.9 %convolution_convert_fusion = bf16[1536,576]{0,1:T(8,128)(2,1)} fusion(bf16[192,1536]{1,0:T(8,128)(2,1)} %copy-done.24, f32[192,576]{1,0:T(8,128)S(1)} %copy-done.6), kind=kOutput, calls=%fused_computation.2 | convolution fusion | flops 340733952 | bytes 2801664 | tf_op jit(solution)/shard_map/dot_general | solution.py:33
  126.6 3.9 %copy.27 = bf16[1536,576]{1,0:T(8,128)(2,1)} copy(bf16[1536,576]{0,1:T(8,128)(2,1)} %convolution_convert_fusion) | data formatting | bytes 3538944 | tf_op jit(solution)/shard_map/convert_element_type | solution.py:161
  130.4 4.5 %reshape.435 = bf16[884736]{0:T(1024)(128)(2,1)} reshape(bf16[1536,576]{1,0:T(8,128)(2,1)} %copy.27) | data formatting | bytes 3538944 | tf_op jit(solution)/shard_map/reshape | solution.py:161
  135.0 3.0 %convolution_convert_fusion.2 = bf16[576,1536]{1,0:T(8,128)(2,1)} fusion(bf16[192,576]{1,0:T(8,128)(2,1)S(1)} %copy-done.10, bf16[192,1536]{1,0:T(8,128)(2,1)} %copy-done.23), kind=kOutput, calls=%fused_computation.4 | convolution fusion | flops 340623360 | bytes 2580480 | tf_op jit(solution)/shard_map/dot_general | solution.py:33
  137.9 4.5 %reshape.433 = bf16[884736]{0:T(1024)(128)(2,1)} reshape(bf16[576,1536]{1,0:T(8,128)(2,1)} %convolution_convert_fusion.2) | data formatting | bytes 3538944 | tf_op jit(solution)/shard_map/reshape | solution.py:161
  142.4 2.9 %convolution_convert_fusion.1 = bf16[576,1536]{1,0:T(8,128)(2,1)} fusion(bf16[192,576]{1,0:T(8,128)(2,1)S(1)} %copy-done.10, bf16[192,1536]{1,0:T(8,128)(2,1)} %copy-done.22), kind=kOutput, calls=%fused_computation.3 | convolution fusion | flops 340623360 | bytes 2580480 | tf_op jit(solution)/shard_map/dot_general | solution.py:33
  145.4 4.5 %reshape.434 = bf16[884736]{0:T(1024)(128)(2,1)} reshape(bf16[576,1536]{1,0:T(8,128)(2,1)} %convolution_convert_fusion.1) | data formatting | bytes 3538944 | tf_op jit(solution)/shard_map/reshape | solution.py:161
  149.8 8.4 %pad_maximum_fusion.1 = bf16[2654208]{0:T(1024)(128)(2,1)} fusion(bf16[884736]{0:T(1024)(128)(2,1)} %reshape.435, bf16[884736]{0:T(1024)(128)(2,1)} %reshape.434, bf16[884736]{0:T(1024)(128)(2,1)} %reshape.433), kind=kLoop, calls=%fused_computation.1 | loop fusion | flops 15925248 | bytes 10616832 | tf_op jit(solution)/shard_map/concatenate | solution.py:161
  158.2 0.5 fusion
  158.8 0.5 fusion.25
  159.3 0.4 copy-done.26
  159.7 0.4 convolution_bitcast_fusion.4
  160.7 0.5 copy-done.13
  161.7 0.6 multiply_reduce_fusion.1
  162.3 0.6 pad_maximum_fusion.7.refs_1_
  162.9 0.9 multiply_add_fusion
  164.3 0.4 reshape.429
  164.6 0.5 convolution_convert_fusion.4
  165.1 0.8 reshape.428
  166.0 5.9 %pad_maximum_fusion = bf16[32,864,128]{2,1,0:T(8,128)(2,1)} fusion(bf16[32,648,128]{2,1,0:T(8,128)(2,1)} %bitcast.141, bf16[32,216,128]{2,1,0:T(8,128)(2,1)S(1)} %bitcast.142), kind=kLoop, calls=%fused_computation | loop fusion | flops 14155776 | bytes 14155776 | tf_op jit(solution)/shard_map/concatenate | solution.py:459
  171.9 51.3 %shard_map.93 = (f32[6,144,128]{2,1,0:T(8,128)}, f32[2,576]{1,0:T(2,128)}) custom-call(bf16[2,2,2,2,2,6,144,128]{7,6,5,4,3,2,1,0:T(8,128)(2,1)} %bitcast.137, f32[2,576]{1,0:T(2,128)} %pad_maximum_fusion.7.refs_1_), custom_call_target="tpu_custom_call" | custom-call | tf_op jit(solution)/shard_map/pallas_call | solution.py:420
  223.2 1.5 slice_bitcast_fusion.1
  224.8 1.7 slice_bitcast_fusion
  226.5 1.3 copy.37
  (90 shorter events, 3.3 us)
Async XLA Ops:
  61.4 3.1 %copy-start.12 = (bf16[576,192]{1,0:T(8,128)(2,1)}, bf16[576,192]{1,0:T(8,128)(2,1)S(1)}, u32[]{:S(2)}) copy-start(bf16[576,192]{1,0:T(8,128)(2,1)S(1)} %reshape.419) | copy-start | bytes 663556
  62.8 7.0 %copy-start.14 = (bf16[576,192]{1,0:T(8,128)(2,1)}, bf16[576,192]{1,0:T(8,128)(2,1)S(1)}, u32[]{:S(2)}) copy-start(bf16[576,192]{1,0:T(8,128)(2,1)S(1)} %reshape.417) | copy-start | bytes 663556
  63.1 9.8 %copy-start.20 = (bf16[192,192]{0,1:T(8,128)(2,1)}, bf16[192,192]{0,1:T(8,128)(2,1)S(1)}, u32[]{:S(2)}) copy-start(bf16[192,192]{0,1:T(8,128)(2,1)S(1)} %convolution_convert_fusion.9) | copy-start | bytes 221188
  70.3 3.1 %copy-start.4 = (bf16[576,576]{1,0:T(8,128)(2,1)}, bf16[576,576]{1,0:T(8,128)(2,1)S(1)}, u32[]{:S(2)}) copy-start(bf16[576,576]{1,0:T(8,128)(2,1)S(1)} %reshape.423) | copy-start | bytes 1990660
  70.9 0.9 copy-start.2
  71.3 0.8 copy-start.30
  71.3 0.8 copy-start.32
  71.3 0.8 copy-start.34
  71.8 0.8 copy-start.27
  71.8 1.1 copy-start.25
  72.6 1.0 copy-start
  73.4 0.8 copy-start.16
  74.2 0.8 copy-start.7
  75.1 26.0 %copy-start.9 = (bf16[192,576]{1,0:T(8,128)(2,1)}, bf16[192,576]{1,0:T(8,128)(2,1)S(1)}, u32[]{:S(2)}) copy-start(bf16[192,576]{1,0:T(8,128)(2,1)S(1)} %multiply_convert_fusion.3) | copy-start | bytes 663556
  85.8 10.7 %copy-start.6 = (f32[192,576]{1,0:T(8,128)S(1)}, f32[192,576]{1,0:T(8,128)}, u32[]{:S(2)}) copy-start(f32[192,576]{1,0:T(8,128)} %param.6) | copy-start | bytes 1327108
  96.5 4.6 %copy-start.1 = (bf16[1728,1536]{1,0:T(8,128)(2,1)S(1)}, bf16[1728,1536]{1,0:T(8,128)(2,1)}, u32[]{:S(2)}) copy-start(bf16[1728,1536]{1,0:T(8,128)(2,1)} %slice.89) | copy-start | bytes 15925252
  101.1 1.0 copy-start.8
  102.1 3.6 %copy-start.24 = (bf16[192,1536]{1,0:T(8,128)(2,1)}, bf16[192,1536]{1,0:T(8,128)(2,1)S(1)}, u32[]{:S(2)}) copy-start(bf16[192,1536]{1,0:T(8,128)(2,1)S(1)} %get-tuple-element.20) | copy-start | bytes 1769476
  102.2 3.6 %copy-start.22 = (bf16[192,1536]{1,0:T(8,128)(2,1)}, bf16[192,1536]{1,0:T(8,128)(2,1)S(1)}, u32[]{:S(2)}) copy-start(bf16[192,1536]{1,0:T(8,128)(2,1)S(1)} %get-tuple-element.21) | copy-start | bytes 1769476
  102.2 4.4 %copy-start.23 = (bf16[192,1536]{1,0:T(8,128)(2,1)}, bf16[192,1536]{1,0:T(8,128)(2,1)S(1)}, u32[]{:S(2)}) copy-start(bf16[192,1536]{1,0:T(8,128)(2,1)S(1)} %get-tuple-element.19) | copy-start | bytes 1769476
  107.5 1.1 copy-start.5
  111.6 1.4 copy-start.15
  130.4 4.5 %copy-start.10 = (bf16[192,576]{1,0:T(8,128)(2,1)S(1)}, bf16[192,576]{1,0:T(8,128)(2,1)}, u32[]{:S(2)}) copy-start(bf16[192,576]{1,0:T(8,128)(2,1)} %copy-done.9) | copy-start | bytes 663556
  149.8 8.4 %copy-start.17 = (bf16[192,576]{0,1:T(8,128)(2,1)S(1)}, bf16[192,576]{0,1:T(8,128)(2,1)}, u32[]{:S(2)}) copy-start(bf16[192,576]{0,1:T(8,128)(2,1)} %copy.21) | copy-start | bytes 663556
  149.8 8.4 %copy-start.21 = (bf16[192,192]{0,1:T(8,128)(2,1)S(1)}, bf16[192,192]{0,1:T(8,128)(2,1)}, u32[]{:S(2)}) copy-start(bf16[192,192]{0,1:T(8,128)(2,1)} %copy-done.20) | copy-start | bytes 221188
  158.7 0.9 copy-start.26
  158.7 1.0 copy-start.28
  158.7 1.4 copy-start.31
  158.7 1.4 copy-start.33
  159.7 0.8 copy-start.29
  160.1 1.0 copy-start.13
  160.5 1.1 copy-start.3
  160.5 1.3 copy-start.18
  164.1 1.8 copy-start.11
  164.1 1.8 copy-start.19

commit v2 on v1

--- a/solution.py
+++ b/solution.py
@@ -6,7 +6,11 @@
 from jax.sharding import PartitionSpec as P
 
 LANES = 128
-PIECES = 6
+ATTN_PIECES = 3
+MLP_PIECES = 9
+PIECES = ATTN_PIECES + MLP_PIECES
+CHUNK = 96
+WIDEN = 288
 MESH = pl.DeviceIdType.MESH
 
 D = 576
@@ -157,10 +161,6 @@
     return (output, kept_state)
 
 
-def flatten(grads):
-    return jnp.concatenate([grad.astype(jnp.bfloat16).ravel() for grad in grads])
-
-
 def mlp_backward(grad_out, kept_state, mlp_weights, gain_rows):
     normed_two, inv_two, entry_two, gate_pre, upward, hidden = kept_state[8:]
     w_gate, w_up, w_down = mlp_weights
@@ -261,15 +261,24 @@
     return tuple(fixed.get(bit, slice(None)) for bit in range(bits - 1, -1, -1))
 
 
-def gather_kernel(bits, shard_ref, full_ref, local_sem, send_sem, recv_sem):
+def locate(piece):
+    return (0, piece // 4) if piece % 4 == 0 else (1, piece - piece // 4 - 1)
+
+
+def gather_kernel(bits, attn_ref, mlp_ref, attn_full, mlp_full, local_sem, send_sem, recv_sem):
     digits, partners = coordinates(bits)
     orders = bit_orders(bits)
-    own = pltpu.make_async_copy(
-        shard_ref, full_ref.at[pick(bits, dict(enumerate(digits)))], local_sem
-    )
-    own.start()
+    fulls = (attn_full, mlp_full)
+    here = pick(bits, dict(enumerate(digits)))
+    own = [
+        pltpu.make_async_copy(shard, full.at[here], local_sem.at[number])
+        for number, (shard, full) in enumerate(zip((attn_ref, mlp_ref), fulls))
+    ]
+    for copy in own:
+        copy.start()
     meet(partners)
-    own.wait()
+    for copy in own:
+        copy.wait()
     flights = {}
     for stage in range(bits):
         for piece in range(PIECES):
@@ -277,7 +286,8 @@
                 flights[piece, stage - 1].wait_recv()
             order = orders[piece]
             fixed = {bit: digits[bit] for bit in order[stage:]}
-            block = full_ref.at[pick(bits, fixed) + (piece,)]
+            array, spot = locate(piece)
+            block = fulls[array].at[pick(bits, fixed) + (spot,)]
             copy = pltpu.make_async_remote_copy(
                 src_ref=block,
                 dst_ref=block,
@@ -294,28 +304,173 @@
         copy.wait_send()
 
 
-def gather(shard):
+def gather(attn_shard, mlp_shard):
     devices = lax.axis_size("dp")
     bits = bit_count(devices)
-    rows = shard.shape[0] // PIECES
-    full = pl.pallas_call(
+    attn = attn_shard.reshape(ATTN_PIECES, -1, LANES)
+    mlp = mlp_shard.reshape(MLP_PIECES, -1, LANES)
+    vmem = pl.BlockSpec(memory_space=pltpu.VMEM)
+    attn_full, mlp_full = pl.pallas_call(
         lambda *refs: gather_kernel(bits, *refs),
-        out_shape=jax.ShapeDtypeStruct((2,) * bits + (PIECES, rows, LANES), shard.dtype),
-        in_specs=[pl.BlockSpec(memory_space=pltpu.VMEM)],
-        out_specs=pl.BlockSpec(memory_space=pltpu.VMEM),
+        out_shape=tuple(
+            jax.ShapeDtypeStruct((2,) * bits + part.shape, part.dtype) for part in (attn, mlp)
+        ),
+        in_specs=[vmem, vmem],
+        out_specs=(vmem, vmem),
         scratch_shapes=[
-            pltpu.SemaphoreType.DMA,
+            pltpu.SemaphoreType.DMA((2,)),
             pltpu.SemaphoreType.DMA((PIECES, bits)),
             pltpu.SemaphoreType.DMA((PIECES, bits)),
         ],
         compiler_params=pltpu.CompilerParams(
             collective_id=0, has_side_effects=True, vmem_limit_bytes=60 << 20
         ),
-    )(shard.reshape(PIECES, rows, LANES))
-    return full.reshape(devices, PIECES * rows, LANES)
-
-
-def scatter_kernel(bits, total_ref, gain_ref, out_ref, gain_out, *scratch):
+    )(attn, mlp)
+    return attn_full.reshape(-1, LANES), mlp_full.reshape(-1, LANES)
+
+
+def strided(start, size, stride):
+    return pl.ds(start, size, stride=stride)
+
+
+def low_half(shape):
+    return lax.broadcasted_iota(jnp.int32, shape, 1) < LANES // 2
+
+
+def swap_halves(block):
+    return pltpu.roll(block, LANES // 2, axis=1)
+
+
+def unflatten_one(flat_ref, first_row, wide, pair, out_ref):
+    rows, columns = out_ref.shape
+    blocks, rest = divmod(columns, LANES)
+
+    @pl.loop(0, rows * columns // LANES // WIDEN)
+    def _(step):
+        start = pl.multiple_of(step * WIDEN, WIDEN)
+        wide[pl.ds(start, WIDEN), :] = flat_ref[pl.ds(first_row + start, WIDEN), :].astype(
+            jnp.float32
+        )
+
+    @pl.loop(0, rows // CHUNK)
+    def _(step):
+        base = step * (CHUNK * columns // LANES)
+        target = pl.ds(pl.multiple_of(step * CHUNK, CHUNK), CHUNK)
+        if rest == 0:
+            for block in range(blocks):
+                out_ref[target, block * LANES : (block + 1) * LANES] = wide[
+                    strided(base + block, CHUNK, blocks), :
+                ].astype(jnp.bfloat16)
+        else:
+            period, half = 2 * blocks + 1, CHUNK // 2
+            lines = [wide[strided(base + line, half, period), :] for line in range(period)]
+            turned = [swap_halves(line) for line in lines[blocks:]]
+            low = low_half((half, LANES))
+            for block in range(blocks + 1):
+                odd = turned[block]
+                if block < blocks:
+                    odd = jnp.where(low, odd, turned[block + 1])
+                pair[block, strided(0, half, 2), :] = lines[block]
+                pair[block, strided(1, half, 2), :] = odd
+            for block in range(blocks):
+                out_ref[target, block * LANES : (block + 1) * LANES] = pair[block].astype(
+                    jnp.bfloat16
+                )
+            out_ref[target, blocks * LANES :] = pair[blocks][:, :rest].astype(jnp.bfloat16)
+
+
+def flatten_one(grad_ref, first_row, wide, pair, flat_ref):
+    rows, columns = grad_ref.shape
+    blocks, rest = divmod(columns, LANES)
+
+    @pl.loop(0, rows // CHUNK)
+    def _(step):
+        base = step * (CHUNK * columns // LANES)
+        origin = pl.ds(pl.multiple_of(step * CHUNK, CHUNK), CHUNK)
+        if rest == 0:
+            for block in range(blocks):
+                wide[strided(base + block, CHUNK, blocks), :] = grad_ref[
+                    origin, block * LANES : (block + 1) * LANES
+                ].astype(jnp.float32)
+        else:
+            period, half = 2 * blocks + 1, CHUNK // 2
+            for block in range(blocks):
+                pair[block] = grad_ref[origin, block * LANES : (block + 1) * LANES].astype(
+                    jnp.float32
+                )
+            tail = grad_ref[origin, blocks * LANES :].astype(jnp.float32)
+            pair[blocks] = jnp.concatenate([tail, tail], axis=1)
+            even = [pair[block, strided(0, half, 2), :] for block in range(blocks + 1)]
+            turned = [
+                swap_halves(pair[block, strided(1, half, 2), :]) for block in range(blocks + 1)
+            ]
+            low = low_half((half, LANES))
+            lines = even[:blocks] + [jnp.where(low, even[blocks], turned[0])]
+            lines += [
+                jnp.where(low, turned[block], turned[block + 1]) for block in range(blocks)
+            ]
+            for line in range(period):
+                wide[strided(base + line, half, period), :] = lines[line]
+
+    @pl.loop(0, rows * columns // LANES // WIDEN)
+    def _(step):
+        start = pl.multiple_of(step * WIDEN, WIDEN)
+        flat_ref[pl.ds(first_row + start, WIDEN), :] = wide[pl.ds(start, WIDEN), :].astype(
+            jnp.bfloat16
+        )
+
+
+KV_WIDTH = KV_HEADS * HEAD_DIM
+ATTN_SHAPES = ((D, D), (D, KV_WIDTH), (D, KV_WIDTH), (D, D))
+MLP_SHAPES = ((D, FF), (D, FF), (FF, D))
+
+
+def relayout_scratch():
+    longest = max(rows * columns for rows, columns in ATTN_SHAPES + MLP_SHAPES) // LANES
+    widest = max(columns for _, columns in ATTN_SHAPES + MLP_SHAPES) // LANES + 1
+    return [
+        pltpu.VMEM((longest, LANES), jnp.float32),
+        pltpu.VMEM((widest, CHUNK, LANES), jnp.float32),
+    ]
+
+
+def relayout(one, shapes, to_flat):
+    def kernel(*refs):
+        wide, pair = refs[-2:]
+        flat_ref = refs[-3] if to_flat else refs[0]
+        matrices = refs[:-3] if to_flat else refs[1:-2]
+        first_row = 0
+        for matrix in matrices:
+            one(*((matrix, first_row, wide, pair, flat_ref) if to_flat else
+                  (flat_ref, first_row, wide, pair, matrix)))
+            first_row += matrix.shape[0] * matrix.shape[1] // LANES
+
+    vmem = pl.BlockSpec(memory_space=pltpu.VMEM)
+    total = sum(rows * columns for rows, columns in shapes) // LANES
+    flat = jax.ShapeDtypeStruct((total, LANES), jnp.bfloat16)
+    many = tuple(jax.ShapeDtypeStruct(shape, jnp.bfloat16) for shape in shapes)
+    return pl.pallas_call(
+        kernel,
+        out_shape=flat if to_flat else many,
+        in_specs=[vmem] * (len(shapes) if to_flat else 1),
+        out_specs=vmem if to_flat else (vmem,) * len(shapes),
+        scratch_shapes=relayout_scratch(),
+        compiler_params=pltpu.CompilerParams(vmem_limit_bytes=40 << 20),
+    )
+
+
+def unflatten(flat, shapes):
+    return relayout(unflatten_one, shapes, False)(flat)
+
+
+def flatten(grads):
+    shapes = tuple(grad.shape for grad in grads)
+    return relayout(flatten_one, shapes, True)(*[grad.astype(jnp.bfloat16) for grad in grads])
+
+
+def scatter_kernel(bits, attn_ref, mlp_ref, gain_ref, attn_out, mlp_out, gain_out, *scratch):
+    totals = (attn_ref, mlp_ref)
+    outs = (attn_out, mlp_out)
     landing = scratch[:bits]
     held = scratch[bits : 2 * bits - 1]
     gain_sent, gain_landing = scratch[2 * bits - 1 : 2 * bits + 1]
@@ -332,15 +487,13 @@
         left = [bit for bit in range(bits - 1, -1, -1) if bit not in order[:stage]]
         return tuple(digit if bit == order[stage] else slice(None) for bit in left)
 
-    def source(piece, stage):
-        return total_ref if stage == 0 else held[stage - 1]
-
     def launch(piece, stage):
         order = orders[piece]
         bit = order[stage]
         lead = block_index(order, stage, 1 - digits[bit])
         if stage == 0:
-            src = total_ref.at[lead + (piece,)]
+            array, place = locate(piece)
+            src = totals[array].at[lead + (place,)]
         else:
             src = held[stage - 1].at[(piece,) + lead]
         copy = pltpu.make_async_remote_copy(
@@ -360,18 +513,19 @@
         bit = order[stage]
         lead = block_index(order, stage, digits[bit])
         free = len(lead) - 1
+        array, slot = locate(piece)
         for number in range(1 << free):
             picks = [(number >> place) & 1 for place in range(free - 1, -1, -1)]
             spot = iter(picks)
             where = tuple(next(spot) if isinstance(item, slice) else item for item in lead)
             if stage == 0:
-                mine = total_ref[where + (piece,)]
+                mine = totals[array][where + (slot,)]
             else:
                 mine = held[stage - 1][(piece,) + where]
             other = landing[stage][(piece,) + tuple(picks)]
             value = mine.astype(jnp.float32) + other.astype(jnp.float32)
             if stage == bits - 1:
-                out_ref[piece] = value
+                outs[array][slot] = value
             else:
                 held[stage][(piece,) + tuple(picks)] = value.astype(jnp.bfloat16)
 
@@ -411,20 +565,23 @@
         copy.wait_send()
 
 
-def scatter(total, gains):
+def scatter(attn_flat, mlp_flat, gains):
     devices = lax.axis_size("dp")
     bits = bit_count(devices)
-    rows = total.shape[1] // PIECES
+    attn = attn_flat.reshape((2,) * bits + (ATTN_PIECES, -1, LANES))
+    mlp = mlp_flat.reshape((2,) * bits + (MLP_PIECES, -1, LANES))
+    rows = mlp.shape[-2]
     slots = [(PIECES,) + (2,) * (bits - 1 - stage) + (rows, LANES) for stage in range(bits)]
     vmem = pl.BlockSpec(memory_space=pltpu.VMEM)
-    out, gain_sum = pl.pallas_call(
+    attn_sum, mlp_sum, gain_sum = pl.pallas_call(
         lambda *refs: scatter_kernel(bits, *refs),
         out_shape=(
-            jax.ShapeDtypeStruct((PIECES, rows, LANES), jnp.float32),
+            jax.ShapeDtypeStruct((ATTN_PIECES, rows, LANES), jnp.float32),
+            jax.ShapeDtypeStruct((MLP_PIECES, rows, LANES), jnp.float32),
             jax.ShapeDtypeStruct(gains.shape, jnp.float32),
         ),
-        in_specs=[vmem, vmem],
-        out_specs=(vmem, vmem),
+        in_specs=[vmem] * 3,
+        out_specs=(vmem,) * 3,
         scratch_shapes=[pltpu.VMEM(slot, jnp.bfloat16) for slot in slots]
         + [pltpu.VMEM(slot, jnp.bfloat16) for slot in slots[:-1]]
         + [
@@ -438,35 +595,21 @@
         compiler_params=pltpu.CompilerParams(
             collective_id=1, has_side_effects=True, vmem_limit_bytes=60 << 20
         ),
-    )(total.reshape((2,) * bits + (PIECES, rows, LANES)), gains)
-    return out.reshape(PIECES * rows, LANES), gain_sum
+    )(attn, mlp, gains)
+    return attn_sum.reshape(-1), mlp_sum.reshape(-1), gain_sum
 
 
 def body(inputs, cotangent, attn_shard, mlp_shard, gain_rows):
-    devices = lax.axis_size("dp")
-    attn_rows = attn_shard.shape[0] // LANES
-    packed = jnp.concatenate(
-        [attn_shard.reshape(-1, LANES), mlp_shard.reshape(-1, LANES)], axis=0
-    )
-    full = gather(packed)
-    attn_weights = split_attention(full[:, :attn_rows].reshape(-1))
-    mlp_weights = split_mlp(full[:, attn_rows:].reshape(-1))
+    attn_full, mlp_full = gather(attn_shard, mlp_shard)
+    attn_weights = unflatten(attn_full, ATTN_SHAPES)
+    mlp_weights = unflatten(mlp_full, MLP_SHAPES)
     outputs, kept_state = forward(inputs, attn_weights, mlp_weights, gain_rows)
     grad_middle, mlp_flat, gain_two = mlp_backward(cotangent, kept_state, mlp_weights, gain_rows)
     grad_input, attn_flat, gain_one = attn_backward(
         grad_middle, kept_state, attn_weights, gain_rows
     )
-    total = jnp.concatenate(
-        [
-            attn_flat.reshape(devices, -1, LANES),
-            mlp_flat.reshape(devices, -1, LANES),
-        ],
-        axis=1,
-    )
     gains = jnp.stack([gain_one, gain_two])
-    summed, gain_grad = scatter(total, gains)
-    attn_grad = summed[:attn_rows].reshape(-1)
-    mlp_grad = summed[attn_rows:].reshape(-1)
+    attn_grad, mlp_grad, gain_grad = scatter(attn_flat, mlp_flat, gains)
     return (outputs, grad_input, attn_grad, mlp_grad, gain_grad)
 
 

time: 230 us -> 168 us (0.73)
  local copies, waits for them, and re-layouts: 66.9 us -> 19.9 us
  other arithmetic: 23.3 us -> 5.48 us
  Pallas kernels: 105 us -> 119 us
  matrix products: 31.7 us -> 21.3 us
    slice x5 -> x0, local copies, waits for them, and re-layouts: 29.1 us -> none  [the longest x1 10.7 us: split_mlp(): flat[2 * edge_one:].reshape(FF, D)]
    reshape x14 -> x0, local copies, waits for them, and re-layouts: 24.3 us -> none  [the longest x7 19.2 us: flatten(): grad.astype(jnp.bfloat16).ravel()]
    concatenate x4 -> x0, other arithmetic: 16 us -> none  [the longest x2 8.48 us: flatten(): jnp.concatenate([grad.astype(jnp.bfloat16).ravel() for grad in grads])]
    pallas_call x1 -> x5, Pallas kernels: 53.3 us -> 66.7 us  [the longest x1 52.2 us: gather(): pl.pallas_call(lambda *refs: gather_kernel(bits, *refs), out_shape=tuple(...]
    unnamed x71 -> x97, local copies, waits for them, and re-layouts: 4.89 us -> 14.2 us
    dot_general x7, matrix products: 12.7 us -> 6.97 us  [inner(): lax.dot_general(left, right, (((0,), (0,)), ((), ())), preferred_element_...]
    dot_general x7, matrix products: 8.22 us -> 4.29 us  [matmul(): return jnp.dot(left, right, preferred_element_type=jnp.float32)]
    convert_element_type x3, local copies, waits for them, and re-layouts: 5.85 us -> 3.05 us  [flatten(): grad.astype(jnp.bfloat16)]
where the time goes in v2:
time: 168 us; the launch traced here: 167 us
  Pallas kernels  119 us (71%)
  matrix products  21.3 us (13%)
  local copies, waits for them, and re-layouts  19.9 us (12%)
  other arithmetic  5.48 us (3%)
    pallas_call x1, Pallas kernels, scatter(): pl.pallas_call(lambda *refs: scatter_kernel(bits, *refs), out_shape=(jax....  52.4 us
    pallas_call x1, Pallas kernels, gather(): pl.pallas_call(lambda *refs: gather_kernel(bits, *refs), out_shape=tuple(...  52.2 us
    unnamed x97, local copies, waits for them, and re-layouts  14.2 us
    pallas_call x2, Pallas kernels, flatten(): relayout(flatten_one, shapes, True)  8.07 us
    dot_general x7, matrix products, inner(): lax.dot_general(left, right, (((0,), (0,)), ((), ())), preferred_element_...  6.97 us
    dot_general x7, matrix products, outer_t(): lax.dot_general(left, right, (((1,), (1,)), ((), ())), preferred_element_...  6.58 us
    pallas_call x2, Pallas kernels, unflatten(): return relayout(unflatten_one, shapes, False)(flat)  6.42 us
    dot_general x7, matrix products, matmul(): return jnp.dot(left, right, preferred_element_type=jnp.float32)  4.29 us

profile of v2, /device:TPU:0, one launch (start us, length us, event | category | flops | bytes accessed | tf_op | source)
XLA Modules:
  0.0 167.1 jit_solution(8523343636416650941)
XLA Ops:
  0.6 0.8 slice_reduce_fusion
  1.4 1.1 multiply_reduce_fusion.5
  2.6 1.1 multiply_convert_fusion.4
  3.7 52.2 %shard_map.92 = (bf16[2,2,2,2,2,3,72,128]{7,6,5,4,3,2,1,0:T(8,128)(2,1)}, bf16[2,2,2,2,2,9,72,128]{7,6,5,4,3,2,1,0:T(8,128)(2,1)}) custom-call(bf16[3,72,128]{2,1,0:T(8,128)(2,1)} %bitcast.157, bf16[9,72,128]{2,1,0:T(8,128)(2,1)} %bitcast.155), custom_call_target="tpu_custom_call" | custom-call | tf_op jit(solution)/shard_map/pallas_call | solution.py:313
  56.0 1.5 copy-done.6
  57.5 2.8 %shard_map.93 = (bf16[576,576]{1,0:T(8,128)(2,1)S(1)}, bf16[576,192]{1,0:T(8,128)(2,1)S(1)}, bf16[576,192]{1,0:T(8,128)(2,1)S(1)}, bf16[576,576]{1,0:T(8,128)(2,1)S(1)}) custom-call(bf16[6912,128]{1,0:T(8,128)(2,1)S(1)} %bitcast.134), custom_call_target="tpu_custom_call" | custom-call | tf_op jit(solution)/shard_map/pallas_call | solution.py:463
  60.3 0.5 fusion.24
  60.8 0.2 fusion.18
  61.0 0.1 subtract_convert_fusion.1
  61.1 0.3 fusion.23
  61.5 0.5 fusion.22
  62.0 0.3 exponential_reduce_fusion
  62.4 0.3 convolution_convert_fusion.9
  62.7 0.4 convolution_convert_fusion.5
  63.1 0.7 copy-done.9
  63.8 0.5 multiply_reduce_fusion.4
  64.3 0.1 multiply_convert_fusion.3
  64.5 3.6 %shard_map.94 = (bf16[576,1536]{1,0:T(8,128)(2,1)S(1)}, bf16[576,1536]{1,0:T(8,128)(2,1)S(1)}, bf16[1536,576]{1,0:T(8,128)(2,1)S(1)}) custom-call(bf16[20736,128]{1,0:T(8,128)(2,1)S(1)} %bitcast.133), custom_call_target="tpu_custom_call" | custom-call | tf_op jit(solution)/shard_map/pallas_call | solution.py:463
  68.1 0.6 fusion.26
  68.8 0.6 fusion.25
  69.4 0.4 copy-done.28
  69.8 1.9 %multiply_convert_fusion = (bf16[192,1536]{1,0:T(8,128)(2,1)S(1)}, bf16[192,1536]{1,0:T(8,128)(2,1)S(1)}, bf16[192,1536]{1,0:T(8,128)(2,1)}) fusion(f32[192,1536]{1,0:T(8,128)S(1)} %fusion.25, f32[192,1536]{1,0:T(8,128)S(1)} %fusion.26, bf16[1536,576]{1,0:T(8,128)(2,1)S(1)} %get-tuple-element.25, f32[192,576]{1,0:T(8,128)S(1)} %copy-done.28), kind=kOutput, calls=%fused_computation.25 | convolution fusion | flops 344567808 | bytes 6340608 | tf_op jit(solution)/shard_map/dot_general | solution.py:43
  71.7 0.8 fusion.27
  72.5 0.9 multiply_reduce_fusion
  73.5 0.2 multiply_add_fusion.1
  73.7 0.8 copy-done.12
  74.4 1.1 convolution_convert_fusion.8
  75.6 1.8 %copy.37 = bf16[192,576]{0,1:T(8,128)(2,1)} copy(bf16[192,576]{1,0:T(8,128)(2,1)} %convolution_convert_fusion.8) | data formatting | bytes 442368 | tf_op jit(solution)/shard_map/convert_element_type | solution.py:195
  77.4 1.5 fusion
  78.9 0.5 fusion.8
  79.4 0.3 copy-done.40
  79.7 0.3 fusion.15
  79.9 0.1 subtract_convert_fusion
  80.1 0.5 copy-done.35
  80.6 0.4 convolution_bitcast_fusion.2
  81.1 0.6 copy-done.32
  81.8 0.3 fusion.28
  82.1 0.4 fusion.6
  82.5 0.3 fusion.29
  82.8 1.3 multiply_reduce_fusion.1
  84.1 0.6 pad_maximum_fusion.5.refs_2_
  84.7 1.9 %convolution_convert_fusion.1.refs_1_ = bf16[576,1536]{1,0:T(8,128)(2,1)} fusion(bf16[192,576]{1,0:T(8,128)(2,1)S(1)} %copy-done.15, bf16[192,1536]{1,0:T(8,128)(2,1)S(1)} %copy-done.22), kind=kOutput, calls=%fused_computation.1 | convolution fusion | flops 340623360 | bytes 2580480 | tf_op jit(solution)/shard_map/dot_general | solution.py:37
  86.6 1.9 %convolution_convert_fusion.2.refs_0_ = bf16[576,1536]{1,0:T(8,128)(2,1)} fusion(bf16[192,576]{1,0:T(8,128)(2,1)S(1)} %copy-done.15, bf16[192,1536]{1,0:T(8,128)(2,1)S(1)} %copy-done.26), kind=kOutput, calls=%fused_computation.2 | convolution fusion | flops 340623360 | bytes 2580480 | tf_op jit(solution)/shard_map/dot_general | solution.py:37
  88.5 1.9 %convolution_convert_fusion = bf16[1536,576]{0,1:T(8,128)(2,1)} fusion(bf16[192,1536]{1,0:T(8,128)(2,1)S(1)} %copy-done.23, f32[192,576]{1,0:T(8,128)S(1)} %copy-done.29), kind=kOutput, calls=%fused_computation | convolution fusion | flops 340733952 | bytes 2801664 | tf_op jit(solution)/shard_map/dot_general | solution.py:37
  90.4 2.7 %copy.43.refs_2_ = bf16[1536,576]{1,0:T(8,128)(2,1)S(1)} copy(bf16[1536,576]{0,1:T(8,128)(2,1)} %convolution_convert_fusion) | data formatting | bytes 3538944 | tf_op jit(solution)/shard_map/convert_element_type | solution.py:468
  93.1 1.5 copy-done.2
  94.6 1.5 copy-done.3
  96.1 4.1 %shard_map.96 = bf16[20736,128]{1,0:T(8,128)(2,1)S(1)} custom-call(bf16[576,1536]{1,0:T(8,128)(2,1)S(1)} %copy-done.3, bf16[576,1536]{1,0:T(8,128)(2,1)S(1)} %copy-done.2, bf16[1536,576]{1,0:T(8,128)(2,1)S(1)} %copy.43.refs_2_), custom_call_target="tpu_custom_call" | custom-call | tf_op jit(solution)/shard_map/pallas_call | solution.py:468
  100.2 2.3 %copy-done = bf16[20736,128]{1,0:T(8,128)(2,1)} copy-done((bf16[20736,128]{1,0:T(8,128)(2,1)}, bf16[20736,128]{1,0:T(8,128)(2,1)S(1)}, u32[]{:S(2)}) %copy-start) | copy-done | bytes 5308440
  102.6 0.4 convolution_convert_fusion.3.refs_3_
  103.0 0.5 convolution_convert_fusion.4.refs_0_
  103.5 0.2 convolution_convert_fusion.7
  103.7 0.2 copy.41.refs_1_
  103.9 0.2 convolution_convert_fusion.6
  104.1 0.2 copy.42.refs_2_
  104.3 4.0 %shard_map.95 = bf16[6912,128]{1,0:T(8,128)(2,1)S(1)} custom-call(bf16[576,576]{1,0:T(8,128)(2,1)S(1)} %convolution_convert_fusion.4.refs_0_, bf16[576,192]{1,0:T(8,128)(2,1)S(1)} %copy.41.refs_1_, bf16[576,192]{1,0:T(8,128)(2,1)S(1)} %copy.42.refs_2_, bf16[576,576]{1,0:T(8,128)(2,1)S(1)} %convolution_convert_fusion.3.refs_3_), custom_call_target="tpu_custom_call" | custom-call | tf_op jit(solution)/shard_map/pallas_call | solution.py:468
  108.3 1.3 copy-done.1
  109.6 52.4 %shard_map.97 = (f32[3,72,128]{2,1,0:T(8,128)}, f32[9,72,128]{2,1,0:T(8,128)}, f32[2,576]{1,0:T(2,128)}) custom-call(bf16[2,2,2,2,2,3,72,128]{7,6,5,4,3,2,1,0:T(8,128)(2,1)} %bitcast.130, bf16[2,2,2,2,2,9,72,128]{7,6,5,4,3,2,1,0:T(8,128)(2,1)} %bitcast.129, f32[2,576]{1,0:T(2,128)} %pad_maximum_fusion.5.refs_2_), custom_call_target="tpu_custom_call" | custom-call | tf_op jit(solution)/shard_map/pallas_call | solution.py:576
  162.0 0.9 multiply_add_fusion
  163.0 0.7 copy-done.5
  163.7 1.4 convolution_add_fusion.3
  165.1 0.7 copy.56
  165.8 0.7 copy.57
  166.6 0.6 copy.58
  (97 shorter events, 0.5 us)
Async XLA Ops:
  56.0 1.5 copy-start.6
  57.4 7.0 %slice-start = ((s8[5308416]{0:T(1024)(128)(4,1)}), s8[1114112]{0:T(1024)(128)(4,1)S(1)}, s32[]{:S(2)}) async-start(s8[5308416]{0:T(1024)(128)(4,1)} %bitcast.131), calls=%async_computation | async-start | bytes 2228224
  61.1 1.2 copy-start.34
  61.1 1.2 copy-start.36
  61.4 0.9 copy-start.39
  61.5 0.9 copy-start.41
  61.5 3.0 %slice-start.1 = ((s8[5308416]{0:T(1024)(128)(4,1)}), s8[4194304]{0:T(1024)(128)(4,1)S(1)}, s32[]{:S(2)}) async-start(s8[5308416]{0:T(1024)(128)(4,1)} %bitcast.131), calls=%async_computation.1 | async-start | bytes 8388608
  62.3 1.4 copy-start.9
  63.1 1.4 copy-start.18
  64.3 9.2 %copy-start.7 = (f32[192,576]{1,0:T(8,128)}, f32[192,576]{1,0:T(8,128)S(1)}, u32[]{:S(2)}) copy-start(f32[192,576]{1,0:T(8,128)S(1)} %get-tuple-element.52) | copy-start | bytes 1327108
  64.4 4.3 %copy-start.14 = (bf16[192,576]{1,0:T(8,128)(2,1)}, bf16[192,576]{1,0:T(8,128)(2,1)S(1)}, u32[]{:S(2)}) copy-start(bf16[192,576]{1,0:T(8,128)(2,1)S(1)} %multiply_convert_fusion.3) | copy-start | bytes 663556
  68.1 1.3 copy-start.4
  68.7 1.1 copy-start.28
  71.7 1.7 %copy-start.21 = (bf16[192,1536]{1,0:T(8,128)(2,1)}, bf16[192,1536]{1,0:T(8,128)(2,1)S(1)}, u32[]{:S(2)}) copy-start(bf16[192,1536]{1,0:T(8,128)(2,1)S(1)} %get-tuple-element.35) | copy-start | bytes 1769476
  71.7 1.7 %copy-start.25 = (bf16[192,1536]{1,0:T(8,128)(2,1)}, bf16[192,1536]{1,0:T(8,128)(2,1)S(1)}, u32[]{:S(2)}) copy-start(bf16[192,1536]{1,0:T(8,128)(2,1)S(1)} %get-tuple-element.36) | copy-start | bytes 1769476
  73.6 0.8 copy-start.12
  78.8 0.8 copy-start.40
  78.8 0.8 copy-start.42
  79.7 0.9 copy-start.35
  79.7 1.0 copy-start.37
  80.0 2.0 %copy-start.20 = (bf16[192,576]{0,1:T(8,128)(2,1)S(1)}, bf16[192,576]{0,1:T(8,128)(2,1)}, u32[]{:S(2)}) copy-start(bf16[192,576]{0,1:T(8,128)(2,1)} %copy.37) | copy-start | bytes 663556
  80.1 2.7 %copy-start.16 = (bf16[1,192,9,64]{1,3,2,0:T(8,128)(2,1)}, bf16[1,192,9,64]{1,3,2,0:T(8,128)(2,1)S(1)}, u32[]{:S(2)}) copy-start(bf16[1,192,9,64]{1,3,2,0:T(8,128)(2,1)S(1)} %pad_maximum_fusion.1) | copy-start | bytes 663556
  81.1 0.6 copy-start.32
  81.8 1.0 copy-start.10
  82.5 1.6 copy-start.30
  82.5 2.2 %copy-start.15 = (bf16[192,576]{1,0:T(8,128)(2,1)S(1)}, bf16[192,576]{1,0:T(8,128)(2,1)}, u32[]{:S(2)}) copy-start(bf16[192,576]{1,0:T(8,128)(2,1)} %copy-done.14) | copy-start | bytes 663556
  82.5 2.2 %copy-start.22 = (bf16[192,1536]{1,0:T(8,128)(2,1)S(1)}, bf16[192,1536]{1,0:T(8,128)(2,1)}, u32[]{:S(2)}) copy-start(bf16[192,1536]{1,0:T(8,128)(2,1)} %copy-done.21) | copy-start | bytes 1769476
  84.1 2.5 %copy-start.26 = (bf16[192,1536]{1,0:T(8,128)(2,1)S(1)}, bf16[192,1536]{1,0:T(8,128)(2,1)}, u32[]{:S(2)}) copy-start(bf16[192,1536]{1,0:T(8,128)(2,1)} %copy-done.25) | copy-start | bytes 1769476
  86.6 1.9 %copy-start.23 = (bf16[192,1536]{1,0:T(8,128)(2,1)S(1)}, bf16[192,1536]{1,0:T(8,128)(2,1)}, u32[]{:S(2)}) copy-start(bf16[192,1536]{1,0:T(8,128)(2,1)} %get-tuple-element.37) | copy-start | bytes 1769476
  86.6 1.9 %copy-start.29 = (f32[192,576]{1,0:T(8,128)S(1)}, f32[192,576]{1,0:T(8,128)}, u32[]{:S(2)}) copy-start(f32[192,576]{1,0:T(8,128)} %param.6) | copy-start | bytes 1327108
  93.1 1.5 copy-start.2
  94.6 1.5 copy-start.3
  96.1 6.5 %copy-start.13 = (f32[192,576]{1,0:T(8,128)S(1)}, f32[192,576]{1,0:T(8,128)}, u32[]{:S(2)}) copy-start(f32[192,576]{1,0:T(8,128)} %copy-done.12) | copy-start | bytes 1327108
  96.1 6.5 %copy-start.19 = (bf16[3,64,3,192]{3,1,2,0:T(8,128)(2,1)S(1)}, bf16[3,64,3,192]{3,1,2,0:T(8,128)(2,1)}, u32[]{:S(2)}) copy-start(bf16[3,64,3,192]{3,1,2,0:T(8,128)(2,1)} %copy-done.18) | copy-start | bytes 663556
  96.1 6.9 %copy-start.17 = (bf16[1,192,9,64]{1,3,2,0:T(8,128)(2,1)S(1)}, bf16[1,192,9,64]{1,3,2,0:T(8,128)(2,1)}, u32[]{:S(2)}) copy-start(bf16[1,192,9,64]{1,3,2,0:T(8,128)(2,1)} %copy-done.16) | copy-start | bytes 663556
  100.2 2.4 %copy-start = (bf16[20736,128]{1,0:T(8,128)(2,1)}, bf16[20736,128]{1,0:T(8,128)(2,1)S(1)}, u32[]{:S(2)}) copy-start(bf16[20736,128]{1,0:T(8,128)(2,1)S(1)} %shard_map.96) | copy-start | bytes 15925252
  102.6 0.9 copy-start.33
  102.6 1.3 copy-start.31
  108.2 1.3 copy-start.1
  109.5 52.5 %copy-start.11 = (f32[192,576]{1,0:T(8,128)S(1)}, f32[192,576]{1,0:T(8,128)}, u32[]{:S(2)}) copy-start(f32[192,576]{1,0:T(8,128)} %param.5) | copy-start | bytes 1327108
  109.5 52.5 %copy-start.27 = (f32[192,576]{1,0:T(8,128)S(1)}, f32[192,576]{1,0:T(8,128)}, u32[]{:S(2)}) copy-start(f32[192,576]{1,0:T(8,128)} %get-tuple-element.56) | copy-start | bytes 1327108
  109.5 53.4 %copy-start.8 = (f32[192,576]{1,0:T(8,128)S(1)}, f32[192,576]{1,0:T(8,128)}, u32[]{:S(2)}) copy-start(f32[192,576]{1,0:T(8,128)} %copy-done.7) | copy-start | bytes 1327108
  109.5 53.4 %copy-start.24 = (bf16[192,1536]{1,0:T(8,128)(2,1)S(1)}, bf16[192,1536]{1,0:T(8,128)(2,1)}, u32[]{:S(2)}) copy-start(bf16[192,1536]{1,0:T(8,128)(2,1)} %get-tuple-element.37) | copy-start | bytes 1769476
  162.0 1.7 %copy-start.5 = (bf16[1536,576]{1,0:T(8,128)(2,1)S(1)}, bf16[1536,576]{1,0:T(8,128)(2,1)}, u32[]{:S(2)}) copy-start(bf16[1536,576]{1,0:T(8,128)(2,1)} %copy-done.4) | copy-start | bytes 5308420
  163.7 1.4 copy-start.43
  163.7 2.1 %copy-start.38 = (f32[9,72,128]{2,1,0:T(8,128)S(1)}, f32[9,72,128]{2,1,0:T(8,128)}, u32[]{:S(2)}) copy-start(f32[9,72,128]{2,1,0:T(8,128)} %get-tuple-element.27) | copy-start | bytes 995332
  163.7 2.8 %copy-start.44 = (f32[2,576]{1,0:T(2,128)S(1)}, f32[2,576]{1,0:T(2,128)}, u32[]{:S(2)}) copy-start(f32[2,576]{1,0:T(2,128)} %get-tuple-element.66) | copy-start | bytes 13828

commit v3 on v2

--- a/solution.py
+++ b/solution.py
@@ -235,12 +235,13 @@
 
 
 def bit_orders(bits):
-    plain = list(range(bits - 1, -1, -1))
-    swapped = list(plain)
-    if bits > 2:
-        first, second = swapped.index(2), swapped.index(1)
-        swapped[first], swapped[second] = swapped[second], swapped[first]
-    return [plain if piece % 2 == 0 else swapped for piece in range(PIECES)]
+    upper = list(range(bits - 1, 2, -1))
+    if bits < 3:
+        return [list(range(bits - 1, -1, -1))] * PIECES
+    late, early = upper + [2, 1, 0], upper + [1, 2, 0]
+    one, two = [1] + upper + [2, 0], [2] + upper + [1, 0]
+    cycle = (late, one, two, early, one, two)
+    return [cycle[piece % len(cycle)] for piece in range(PIECES)]
 
 
 def coordinates(bits):
@@ -323,7 +324,7 @@
             pltpu.SemaphoreType.DMA((PIECES, bits)),
         ],
         compiler_params=pltpu.CompilerParams(
-            collective_id=0, has_side_effects=True, vmem_limit_bytes=60 << 20
+            collective_id=0, has_side_effects=True, vmem_limit_bytes=16 << 20
         ),
     )(attn, mlp)
     return attn_full.reshape(-1, LANES), mlp_full.reshape(-1, LANES)
@@ -455,7 +456,7 @@
         in_specs=[vmem] * (len(shapes) if to_flat else 1),
         out_specs=vmem if to_flat else (vmem,) * len(shapes),
         scratch_shapes=relayout_scratch(),
-        compiler_params=pltpu.CompilerParams(vmem_limit_bytes=40 << 20),
+        compiler_params=pltpu.CompilerParams(vmem_limit_bytes=20 << 20),
     )
 
 
@@ -593,7 +594,7 @@
             pltpu.SemaphoreType.DMA((bits,)),
         ],
         compiler_params=pltpu.CompilerParams(
-            collective_id=1, has_side_effects=True, vmem_limit_bytes=60 << 20
+            collective_id=1, has_side_effects=True, vmem_limit_bytes=32 << 20
         ),
     )(attn, mlp, gains)
     return attn_sum.reshape(-1), mlp_sum.reshape(-1), gain_sum

time: 168 us -> 157 us (0.935)
  Pallas kernels: 119 us -> 107 us
    pallas_call x1, Pallas kernels: 52.2 us -> 45.4 us  [gather(): pl.pallas_call(lambda *refs: gather_kernel(bits, *refs), out_shape=tuple(...]
    pallas_call x1, Pallas kernels: 52.4 us -> 47.5 us  [scatter(): pl.pallas_call(lambda *refs: scatter_kernel(bits, *refs), out_shape=(jax....]
    unnamed x97 -> x89, local copies, waits for them, and re-layouts: 14.2 us -> 15.8 us
where the time goes in v3:
time: 157 us; the launch traced here: 156 us
  Pallas kernels  107 us (68%)
  local copies, waits for them, and re-layouts  21.5 us (14%)
  matrix products  21.4 us (14%)
  other arithmetic  4.9 us (3%)
    pallas_call x1, Pallas kernels, scatter(): pl.pallas_call(lambda *refs: scatter_kernel(bits, *refs), out_shape=(jax....  47.5 us
    pallas_call x1, Pallas kernels, gather(): pl.pallas_call(lambda *refs: gather_kernel(bits, *refs), out_shape=tuple(...  45.4 us
    unnamed x89, local copies, waits for them, and re-layouts  15.8 us
    pallas_call x2, Pallas kernels, flatten(): relayout(flatten_one, shapes, True)  8.07 us
    dot_general x7, matrix products, inner(): lax.dot_general(left, right, (((0,), (0,)), ((), ())), preferred_element_...  7.01 us
    dot_general x7, matrix products, outer_t(): lax.dot_general(left, right, (((1,), (1,)), ((), ())), preferred_element_...  6.65 us
    pallas_call x2, Pallas kernels, unflatten(): return relayout(unflatten_one, shapes, False)(flat)  6.43 us
    dot_general x7, matrix products, matmul(): return jnp.dot(left, right, preferred_element_type=jnp.float32)  4.3 us

profile of v3, /device:TPU:0, one launch (start us, length us, event | category | flops | bytes accessed | tf_op | source)
XLA Modules:
  0.0 156.5 jit_solution(13320865612377318945)
XLA Ops:
  0.6 0.8 slice_reduce_fusion
  1.4 1.1 multiply_reduce_fusion.5
  2.6 1.1 multiply_convert_fusion.4
  3.7 0.9 copy-done.6
  4.7 0.8 copy-done.7
  5.5 45.4 %shard_map.92 = (bf16[2,2,2,2,2,3,72,128]{7,6,5,4,3,2,1,0:T(8,128)(2,1)S(1)}, bf16[2,2,2,2,2,9,72,128]{7,6,5,4,3,2,1,0:T(8,128)(2,1)S(1)}) custom-call(bf16[3,72,128]{2,1,0:T(8,128)(2,1)S(1)} %bitcast.136, bf16[9,72,128]{2,1,0:T(8,128)(2,1)S(1)} %bitcast.134), custom_call_target="tpu_custom_call" | custom-call | tf_op jit(solution)/shard_map/pallas_call | solution.py:314
  50.9 2.8 %shard_map.93 = (bf16[576,576]{1,0:T(8,128)(2,1)S(1)}, bf16[576,192]{1,0:T(8,128)(2,1)S(1)}, bf16[576,192]{1,0:T(8,128)(2,1)S(1)}, bf16[576,576]{1,0:T(8,128)(2,1)S(1)}) custom-call(bf16[6912,128]{1,0:T(8,128)(2,1)S(1)} %bitcast.132), custom_call_target="tpu_custom_call" | custom-call | tf_op jit(solution)/shard_map/pallas_call | solution.py:464
  53.8 0.5 fusion.24
  54.2 0.2 fusion.18
  54.5 0.3 fusion.23
  55.0 0.2 copy-done.35
  55.2 0.5 fusion.22
  55.7 0.3 exponential_reduce_fusion
  56.0 0.3 convolution_convert_fusion.9
  56.4 0.4 convolution_convert_fusion.5
  56.8 0.3 copy-done.10
  57.0 0.5 multiply_reduce_fusion.4
  57.6 0.1 multiply_convert_fusion.3
  57.7 3.6 %shard_map.94 = (bf16[576,1536]{1,0:T(8,128)(2,1)S(1)}, bf16[576,1536]{1,0:T(8,128)(2,1)S(1)}, bf16[1536,576]{1,0:T(8,128)(2,1)S(1)}) custom-call(bf16[20736,128]{1,0:T(8,128)(2,1)S(1)} %bitcast.131), custom_call_target="tpu_custom_call" | custom-call | tf_op jit(solution)/shard_map/pallas_call | solution.py:464
  61.3 0.6 fusion.26
  62.0 0.6 fusion.25
  62.6 0.4 copy-done.29
  63.0 1.9 %multiply_convert_fusion = (bf16[192,1536]{1,0:T(8,128)(2,1)S(1)}, bf16[192,1536]{1,0:T(8,128)(2,1)S(1)}, bf16[192,1536]{1,0:T(8,128)(2,1)}) fusion(f32[192,1536]{1,0:T(8,128)S(1)} %fusion.25, f32[192,1536]{1,0:T(8,128)S(1)} %fusion.26, bf16[1536,576]{1,0:T(8,128)(2,1)S(1)} %get-tuple-element.25, f32[192,576]{1,0:T(8,128)S(1)} %copy-done.29), kind=kOutput, calls=%fused_computation.25 | convolution fusion | flops 344567808 | bytes 6340608 | tf_op jit(solution)/shard_map/dot_general | solution.py:43
  64.9 0.8 fusion.27
  65.7 1.0 multiply_reduce_fusion
  66.7 0.2 multiply_add_fusion.1
  66.9 0.8 copy-done.13
  67.7 1.2 convolution_convert_fusion.8
  68.8 1.8 %copy.37 = bf16[192,576]{0,1:T(8,128)(2,1)} copy(bf16[192,576]{1,0:T(8,128)(2,1)} %convolution_convert_fusion.8) | data formatting | bytes 442368 | tf_op jit(solution)/shard_map/convert_element_type | solution.py:195
  70.7 1.5 fusion
  72.1 0.5 fusion.8
  72.7 0.3 copy-done.40
  72.9 0.3 fusion.15
  73.4 0.5 copy-done.36
  73.9 0.4 convolution_bitcast_fusion.2
  74.4 0.6 copy-done.33
  75.0 0.3 fusion.28
  75.3 0.4 fusion.6
  75.8 0.3 fusion.29
  76.1 0.3 copy-done.31
  76.4 1.3 multiply_reduce_fusion.1
  77.8 1.9 %convolution_convert_fusion.1.refs_1_ = bf16[576,1536]{1,0:T(8,128)(2,1)} fusion(bf16[192,576]{1,0:T(8,128)(2,1)S(1)} %copy-done.16, bf16[192,1536]{1,0:T(8,128)(2,1)S(1)} %copy-done.23), kind=kOutput, calls=%fused_computation.1 | convolution fusion | flops 340623360 | bytes 2580480 | tf_op jit(solution)/shard_map/dot_general | solution.py:37
  79.7 1.9 %convolution_convert_fusion.2.refs_0_ = bf16[576,1536]{1,0:T(8,128)(2,1)} fusion(bf16[192,576]{1,0:T(8,128)(2,1)S(1)} %copy-done.16, bf16[192,1536]{1,0:T(8,128)(2,1)S(1)} %copy-done.27), kind=kOutput, calls=%fused_computation.2 | convolution fusion | flops 340623360 | bytes 2580480 | tf_op jit(solution)/shard_map/dot_general | solution.py:37
  81.6 1.9 %convolution_convert_fusion = bf16[1536,576]{0,1:T(8,128)(2,1)} fusion(bf16[192,1536]{1,0:T(8,128)(2,1)S(1)} %copy-done.24, f32[192,576]{1,0:T(8,128)S(1)} %copy-done.30), kind=kOutput, calls=%fused_computation | convolution fusion | flops 340733952 | bytes 2801664 | tf_op jit(solution)/shard_map/dot_general | solution.py:37
  83.5 2.7 %copy.43.refs_2_ = bf16[1536,576]{1,0:T(8,128)(2,1)S(1)} copy(bf16[1536,576]{0,1:T(8,128)(2,1)} %convolution_convert_fusion) | data formatting | bytes 3538944 | tf_op jit(solution)/shard_map/convert_element_type | solution.py:469
  86.2 1.5 copy-done.2
  87.7 1.5 copy-done.3
  89.2 4.1 %shard_map.96 = bf16[20736,128]{1,0:T(8,128)(2,1)S(1)} custom-call(bf16[576,1536]{1,0:T(8,128)(2,1)S(1)} %copy-done.3, bf16[576,1536]{1,0:T(8,128)(2,1)S(1)} %copy-done.2, bf16[1536,576]{1,0:T(8,128)(2,1)S(1)} %copy.43.refs_2_), custom_call_target="tpu_custom_call" | custom-call | tf_op jit(solution)/shard_map/pallas_call | solution.py:469
  93.3 2.3 %copy-done = bf16[20736,128]{1,0:T(8,128)(2,1)} copy-done((bf16[20736,128]{1,0:T(8,128)(2,1)}, bf16[20736,128]{1,0:T(8,128)(2,1)S(1)}, u32[]{:S(2)}) %copy-start) | copy-done | bytes 5308440
  95.7 0.4 convolution_convert_fusion.3.refs_3_
  96.1 0.5 convolution_convert_fusion.4.refs_0_
  96.5 0.2 convolution_convert_fusion.7
  96.8 0.2 copy.41.refs_1_
  96.9 0.2 convolution_convert_fusion.6
  97.2 0.2 copy.42.refs_2_
  97.3 4.0 %shard_map.95 = bf16[6912,128]{1,0:T(8,128)(2,1)S(1)} custom-call(bf16[576,576]{1,0:T(8,128)(2,1)S(1)} %convolution_convert_fusion.4.refs_0_, bf16[576,192]{1,0:T(8,128)(2,1)S(1)} %copy.41.refs_1_, bf16[576,192]{1,0:T(8,128)(2,1)S(1)} %copy.42.refs_2_, bf16[576,576]{1,0:T(8,128)(2,1)S(1)} %convolution_convert_fusion.3.refs_3_), custom_call_target="tpu_custom_call" | custom-call | tf_op jit(solution)/shard_map/pallas_call | solution.py:469
  101.3 2.5 %copy-done.1 = bf16[20736,128]{1,0:T(8,128)(2,1)S(1)} copy-done((bf16[20736,128]{1,0:T(8,128)(2,1)S(1)}, bf16[20736,128]{1,0:T(8,128)(2,1)}, u32[]{:S(2)}) %copy-start.1) | copy-done | bytes 5308440
  103.8 47.5 %shard_map.97 = (f32[3,72,128]{2,1,0:T(8,128)S(1)}, f32[9,72,128]{2,1,0:T(8,128)S(1)}, f32[2,576]{1,0:T(2,128)S(1)}) custom-call(bf16[2,2,2,2,2,3,72,128]{7,6,5,4,3,2,1,0:T(8,128)(2,1)S(1)} %bitcast.130, bf16[2,2,2,2,2,9,72,128]{7,6,5,4,3,2,1,0:T(8,128)(2,1)S(1)} %bitcast.129, f32[2,576]{1,0:T(2,128)S(1)} %pad_maximum_fusion.5.refs_2_), custom_call_target="tpu_custom_call" | custom-call | tf_op jit(solution)/shard_map/pallas_call | solution.py:577
  151.4 0.9 multiply_add_fusion
  152.3 0.7 copy-done.5
  153.0 1.4 convolution_add_fusion.3
  154.5 0.7 copy.56
  155.1 0.7 copy.57
  155.9 0.6 copy.58
  (88 shorter events, 0.6 us)
Async XLA Ops:
  3.7 0.9 copy-start.6
  4.7 0.8 copy-start.7
  54.5 0.7 copy-start.35
  54.5 1.1 copy-start.37
  54.9 1.1 copy-start.39
  54.9 1.1 copy-start.41
  56.0 1.0 copy-start.10
  56.8 0.9 copy-start.19
  57.5 9.2 %copy-start.8 = (f32[192,576]{1,0:T(8,128)}, f32[192,576]{1,0:T(8,128)S(1)}, u32[]{:S(2)}) copy-start(f32[192,576]{1,0:T(8,128)S(1)} %get-tuple-element.52) | copy-start | bytes 1327108
  57.7 4.3 %copy-start.15 = (bf16[192,576]{1,0:T(8,128)(2,1)}, bf16[192,576]{1,0:T(8,128)(2,1)S(1)}, u32[]{:S(2)}) copy-start(bf16[192,576]{1,0:T(8,128)(2,1)S(1)} %multiply_convert_fusion.3) | copy-start | bytes 663556
  61.3 1.3 copy-start.4
  61.9 1.1 copy-start.29
  64.9 1.8 %copy-start.22 = (bf16[192,1536]{1,0:T(8,128)(2,1)}, bf16[192,1536]{1,0:T(8,128)(2,1)S(1)}, u32[]{:S(2)}) copy-start(bf16[192,1536]{1,0:T(8,128)(2,1)S(1)} %get-tuple-element.35) | copy-start | bytes 1769476
  64.9 1.8 %copy-start.26 = (bf16[192,1536]{1,0:T(8,128)(2,1)}, bf16[192,1536]{1,0:T(8,128)(2,1)S(1)}, u32[]{:S(2)}) copy-start(bf16[192,1536]{1,0:T(8,128)(2,1)S(1)} %get-tuple-element.36) | copy-start | bytes 1769476
  66.9 0.8 copy-start.13
  72.1 0.8 copy-start.40
  72.1 0.8 copy-start.42
  72.9 0.9 copy-start.36
  72.9 1.0 copy-start.38
  73.3 2.0 %copy-start.21 = (bf16[192,576]{0,1:T(8,128)(2,1)S(1)}, bf16[192,576]{0,1:T(8,128)(2,1)}, u32[]{:S(2)}) copy-start(bf16[192,576]{0,1:T(8,128)(2,1)} %copy.37) | copy-start | bytes 663556
  73.4 2.7 %copy-start.17 = (bf16[1,192,9,64]{1,3,2,0:T(8,128)(2,1)}, bf16[1,192,9,64]{1,3,2,0:T(8,128)(2,1)S(1)}, u32[]{:S(2)}) copy-start(bf16[1,192,9,64]{1,3,2,0:T(8,128)(2,1)S(1)} %pad_maximum_fusion.1) | copy-start | bytes 663556
  74.4 0.6 copy-start.33
  75.0 1.4 copy-start.11
  75.8 0.6 copy-start.31
  75.8 2.0 %copy-start.16 = (bf16[192,576]{1,0:T(8,128)(2,1)S(1)}, bf16[192,576]{1,0:T(8,128)(2,1)}, u32[]{:S(2)}) copy-start(bf16[192,576]{1,0:T(8,128)(2,1)} %copy-done.15) | copy-start | bytes 663556
  75.8 2.0 %copy-start.23 = (bf16[192,1536]{1,0:T(8,128)(2,1)S(1)}, bf16[192,1536]{1,0:T(8,128)(2,1)}, u32[]{:S(2)}) copy-start(bf16[192,1536]{1,0:T(8,128)(2,1)} %copy-done.22) | copy-start | bytes 1769476
  77.7 2.0 %copy-start.27 = (bf16[192,1536]{1,0:T(8,128)(2,1)S(1)}, bf16[192,1536]{1,0:T(8,128)(2,1)}, u32[]{:S(2)}) copy-start(bf16[192,1536]{1,0:T(8,128)(2,1)} %copy-done.26) | copy-start | bytes 1769476
  79.7 1.9 %copy-start.24 = (bf16[192,1536]{1,0:T(8,128)(2,1)S(1)}, bf16[192,1536]{1,0:T(8,128)(2,1)}, u32[]{:S(2)}) copy-start(bf16[192,1536]{1,0:T(8,128)(2,1)} %get-tuple-element.37) | copy-start | bytes 1769476
  79.7 1.9 %copy-start.30 = (f32[192,576]{1,0:T(8,128)S(1)}, f32[192,576]{1,0:T(8,128)}, u32[]{:S(2)}) copy-start(f32[192,576]{1,0:T(8,128)} %param.6) | copy-start | bytes 1327108
  86.2 1.5 copy-start.2
  87.7 1.5 copy-start.3
  89.2 6.5 %copy-start.14 = (f32[192,576]{1,0:T(8,128)S(1)}, f32[192,576]{1,0:T(8,128)}, u32[]{:S(2)}) copy-start(f32[192,576]{1,0:T(8,128)} %copy-done.13) | copy-start | bytes 1327108
  89.2 6.5 %copy-start.20 = (bf16[3,64,3,192]{3,1,2,0:T(8,128)(2,1)S(1)}, bf16[3,64,3,192]{3,1,2,0:T(8,128)(2,1)}, u32[]{:S(2)}) copy-start(bf16[3,64,3,192]{3,1,2,0:T(8,128)(2,1)} %copy-done.19) | copy-start | bytes 663556
  89.2 6.9 %copy-start.18 = (bf16[1,192,9,64]{1,3,2,0:T(8,128)(2,1)S(1)}, bf16[1,192,9,64]{1,3,2,0:T(8,128)(2,1)}, u32[]{:S(2)}) copy-start(bf16[1,192,9,64]{1,3,2,0:T(8,128)(2,1)} %copy-done.17) | copy-start | bytes 663556
  93.3 2.3 %copy-start = (bf16[20736,128]{1,0:T(8,128)(2,1)}, bf16[20736,128]{1,0:T(8,128)(2,1)S(1)}, u32[]{:S(2)}) copy-start(bf16[20736,128]{1,0:T(8,128)(2,1)S(1)} %shard_map.96) | copy-start | bytes 15925252
  95.6 0.9 copy-start.34
  95.6 1.3 copy-start.32
  101.3 2.5 %copy-start.1 = (bf16[20736,128]{1,0:T(8,128)(2,1)S(1)}, bf16[20736,128]{1,0:T(8,128)(2,1)}, u32[]{:S(2)}) copy-start(bf16[20736,128]{1,0:T(8,128)(2,1)} %copy-done) | copy-start | bytes 15925252
  103.8 47.5 %copy-start.12 = (f32[192,576]{1,0:T(8,128)S(1)}, f32[192,576]{1,0:T(8,128)}, u32[]{:S(2)}) copy-start(f32[192,576]{1,0:T(8,128)} %param.5) | copy-start | bytes 1327108
  103.8 47.5 %copy-start.28 = (f32[192,576]{1,0:T(8,128)S(1)}, f32[192,576]{1,0:T(8,128)}, u32[]{:S(2)}) copy-start(f32[192,576]{1,0:T(8,128)} %get-tuple-element.56) | copy-start | bytes 1327108
  103.8 48.5 %copy-start.9 = (f32[192,576]{1,0:T(8,128)S(1)}, f32[192,576]{1,0:T(8,128)}, u32[]{:S(2)}) copy-start(f32[192,576]{1,0:T(8,128)} %copy-done.8) | copy-start | bytes 1327108
  103.8 48.5 %copy-start.25 = (bf16[192,1536]{1,0:T(8,128)(2,1)S(1)}, bf16[192,1536]{1,0:T(8,128)(2,1)}, u32[]{:S(2)}) copy-start(bf16[192,1536]{1,0:T(8,128)(2,1)} %get-tuple-element.37) | copy-start | bytes 1769476
  151.3 1.7 %copy-start.5 = (bf16[1536,576]{1,0:T(8,128)(2,1)S(1)}, bf16[1536,576]{1,0:T(8,128)(2,1)}, u32[]{:S(2)}) copy-start(bf16[1536,576]{1,0:T(8,128)(2,1)} %copy-done.4) | copy-start | bytes 5308420

commit v4 on v3

--- a/solution.py
+++ b/solution.py
@@ -244,6 +244,22 @@
     return [cycle[piece % len(cycle)] for piece in range(PIECES)]
 
 
+GROUP = 3
+
+
+def waves(bits):
+    groups = PIECES // GROUP
+    return [
+        [
+            (group * GROUP + member, step - group)
+            for group in range(groups)
+            if 0 <= step - group < bits
+            for member in range(GROUP)
+        ]
+        for step in range(bits + groups - 1)
+    ]
+
+
 def coordinates(bits):
     me = lax.axis_index("dp")
     digits = [lax.rem(me // (1 << bit), 2) for bit in range(bits)]
@@ -281,8 +297,8 @@
     for copy in own:
         copy.wait()
     flights = {}
-    for stage in range(bits):
-        for piece in range(PIECES):
+    for wave in waves(bits):
+        for piece, stage in wave:
             if stage > 0:
                 flights[piece, stage - 1].wait_recv()
             order = orders[piece]
@@ -551,11 +567,12 @@
         else:
             gain_sent[stage + 1] = value
 
-    for stage in range(bits):
-        if stage > 0:
-            absorb_gain(stage - 1)
-        launch_gain(stage)
-        for piece in range(PIECES):
+    for step, wave in enumerate(waves(bits)):
+        if 0 < step < bits:
+            absorb_gain(step - 1)
+        if step < bits:
+            launch_gain(step)
+        for piece, stage in wave:
             if stage > 0:
                 absorb(piece, stage - 1)
             launch(piece, stage)

time: 157 us -> 160 us (1.019)
  Pallas kernels: 107 us -> 110 us
    pallas_call x1, Pallas kernels: 45.4 us -> 48 us  [gather(): pl.pallas_call(lambda *refs: gather_kernel(bits, *refs), out_shape=tuple(...]
where the time goes in v4:
time: 160 us; the launch traced here: 159 us
  Pallas kernels  110 us (69%)
  local copies, waits for them, and re-layouts  21.5 us (13%)
  matrix products  21.4 us (13%)
  other arithmetic  4.9 us (3%)
    pallas_call x1, Pallas kernels, gather(): pl.pallas_call(lambda *refs: gather_kernel(bits, *refs), out_shape=tuple(...  48 us
    pallas_call x1, Pallas kernels, scatter(): pl.pallas_call(lambda *refs: scatter_kernel(bits, *refs), out_shape=(jax....  47.7 us
    unnamed x89, local copies, waits for them, and re-layouts  15.8 us
    pallas_call x2, Pallas kernels, flatten(): relayout(flatten_one, shapes, True)  8.07 us
    dot_general x7, matrix products, inner(): lax.dot_general(left, right, (((0,), (0,)), ((), ())), preferred_element_...  7.01 us
    dot_general x7, matrix products, outer_t(): lax.dot_general(left, right, (((1,), (1,)), ((), ())), preferred_element_...  6.65 us
    pallas_call x2, Pallas kernels, unflatten(): return relayout(unflatten_one, shapes, False)(flat)  6.43 us
    dot_general x7, matrix products, matmul(): return jnp.dot(left, right, preferred_element_type=jnp.float32)  4.31 us

profile of v4, /device:TPU:0, one launch (start us, length us, event | category | flops | bytes accessed | tf_op | source)
XLA Modules:
  0.0 159.3 jit_solution(15843418203486127995)
XLA Ops:
  0.6 0.8 slice_reduce_fusion
  1.4 1.1 multiply_reduce_fusion.5
  2.6 1.1 multiply_convert_fusion.4
  3.7 0.9 copy-done.6
  4.7 0.8 copy-done.7
  5.5 48.0 %shard_map.92 = (bf16[2,2,2,2,2,3,72,128]{7,6,5,4,3,2,1,0:T(8,128)(2,1)S(1)}, bf16[2,2,2,2,2,9,72,128]{7,6,5,4,3,2,1,0:T(8,128)(2,1)S(1)}) custom-call(bf16[3,72,128]{2,1,0:T(8,128)(2,1)S(1)} %bitcast.136, bf16[9,72,128]{2,1,0:T(8,128)(2,1)S(1)} %bitcast.134), custom_call_target="tpu_custom_call" | custom-call | tf_op jit(solution)/shard_map/pallas_call | solution.py:330
  53.4 2.8 %shard_map.93 = (bf16[576,576]{1,0:T(8,128)(2,1)S(1)}, bf16[576,192]{1,0:T(8,128)(2,1)S(1)}, bf16[576,192]{1,0:T(8,128)(2,1)S(1)}, bf16[576,576]{1,0:T(8,128)(2,1)S(1)}) custom-call(bf16[6912,128]{1,0:T(8,128)(2,1)S(1)} %bitcast.132), custom_call_target="tpu_custom_call" | custom-call | tf_op jit(solution)/shard_map/pallas_call | solution.py:480
  56.3 0.5 fusion.24
  56.8 0.2 fusion.18
  57.1 0.3 fusion.23
  57.5 0.2 copy-done.35
  57.7 0.5 fusion.22
  58.2 0.3 exponential_reduce_fusion
  58.6 0.3 convolution_convert_fusion.9
  58.9 0.4 convolution_convert_fusion.5
  59.3 0.3 copy-done.10
  59.6 0.5 multiply_reduce_fusion.4
  60.1 0.1 multiply_convert_fusion.3
  60.2 3.6 %shard_map.94 = (bf16[576,1536]{1,0:T(8,128)(2,1)S(1)}, bf16[576,1536]{1,0:T(8,128)(2,1)S(1)}, bf16[1536,576]{1,0:T(8,128)(2,1)S(1)}) custom-call(bf16[20736,128]{1,0:T(8,128)(2,1)S(1)} %bitcast.131), custom_call_target="tpu_custom_call" | custom-call | tf_op jit(solution)/shard_map/pallas_call | solution.py:480
  63.9 0.6 fusion.26
  64.5 0.6 fusion.25
  65.2 0.4 copy-done.29
  65.5 1.9 %multiply_convert_fusion = (bf16[192,1536]{1,0:T(8,128)(2,1)S(1)}, bf16[192,1536]{1,0:T(8,128)(2,1)S(1)}, bf16[192,1536]{1,0:T(8,128)(2,1)}) fusion(f32[192,1536]{1,0:T(8,128)S(1)} %fusion.25, f32[192,1536]{1,0:T(8,128)S(1)} %fusion.26, bf16[1536,576]{1,0:T(8,128)(2,1)S(1)} %get-tuple-element.25, f32[192,576]{1,0:T(8,128)S(1)} %copy-done.29), kind=kOutput, calls=%fused_computation.25 | convolution fusion | flops 344567808 | bytes 6340608 | tf_op jit(solution)/shard_map/dot_general | solution.py:43
  67.4 0.8 fusion.27
  68.2 1.0 multiply_reduce_fusion
  69.2 0.2 multiply_add_fusion.1
  69.5 0.8 copy-done.13
  70.2 1.2 convolution_convert_fusion.8
  71.4 1.8 %copy.37 = bf16[192,576]{0,1:T(8,128)(2,1)} copy(bf16[192,576]{1,0:T(8,128)(2,1)} %convolution_convert_fusion.8) | data formatting | bytes 442368 | tf_op jit(solution)/shard_map/convert_element_type | solution.py:195
  73.2 1.5 fusion
  74.7 0.5 fusion.8
  75.2 0.3 copy-done.40
  75.5 0.3 fusion.15
  75.9 0.5 copy-done.36
  76.5 0.4 convolution_bitcast_fusion.2
  77.0 0.6 copy-done.33
  77.6 0.3 fusion.28
  77.9 0.4 fusion.6
  78.3 0.3 fusion.29
  78.6 0.3 copy-done.31
  79.0 1.3 multiply_reduce_fusion.1
  80.3 1.9 %convolution_convert_fusion.1.refs_1_ = bf16[576,1536]{1,0:T(8,128)(2,1)} fusion(bf16[192,576]{1,0:T(8,128)(2,1)S(1)} %copy-done.16, bf16[192,1536]{1,0:T(8,128)(2,1)S(1)} %copy-done.23), kind=kOutput, calls=%fused_computation.1 | convolution fusion | flops 340623360 | bytes 2580480 | tf_op jit(solution)/shard_map/dot_general | solution.py:37
  82.2 1.9 %convolution_convert_fusion.2.refs_0_ = bf16[576,1536]{1,0:T(8,128)(2,1)} fusion(bf16[192,576]{1,0:T(8,128)(2,1)S(1)} %copy-done.16, bf16[192,1536]{1,0:T(8,128)(2,1)S(1)} %copy-done.27), kind=kOutput, calls=%fused_computation.2 | convolution fusion | flops 340623360 | bytes 2580480 | tf_op jit(solution)/shard_map/dot_general | solution.py:37
  84.1 1.9 %convolution_convert_fusion = bf16[1536,576]{0,1:T(8,128)(2,1)} fusion(bf16[192,1536]{1,0:T(8,128)(2,1)S(1)} %copy-done.24, f32[192,576]{1,0:T(8,128)S(1)} %copy-done.30), kind=kOutput, calls=%fused_computation | convolution fusion | flops 340733952 | bytes 2801664 | tf_op jit(solution)/shard_map/dot_general | solution.py:37
  86.0 2.7 %copy.43.refs_2_ = bf16[1536,576]{1,0:T(8,128)(2,1)S(1)} copy(bf16[1536,576]{0,1:T(8,128)(2,1)} %convolution_convert_fusion) | data formatting | bytes 3538944 | tf_op jit(solution)/shard_map/convert_element_type | solution.py:485
  88.8 1.5 copy-done.2
  90.2 1.5 copy-done.3
  91.7 4.1 %shard_map.96 = bf16[20736,128]{1,0:T(8,128)(2,1)S(1)} custom-call(bf16[576,1536]{1,0:T(8,128)(2,1)S(1)} %copy-done.3, bf16[576,1536]{1,0:T(8,128)(2,1)S(1)} %copy-done.2, bf16[1536,576]{1,0:T(8,128)(2,1)S(1)} %copy.43.refs_2_), custom_call_target="tpu_custom_call" | custom-call | tf_op jit(solution)/shard_map/pallas_call | solution.py:485
  95.8 2.3 %copy-done = bf16[20736,128]{1,0:T(8,128)(2,1)} copy-done((bf16[20736,128]{1,0:T(8,128)(2,1)}, bf16[20736,128]{1,0:T(8,128)(2,1)S(1)}, u32[]{:S(2)}) %copy-start) | copy-done | bytes 5308440
  98.2 0.4 convolution_convert_fusion.3.refs_3_
  98.6 0.5 convolution_convert_fusion.4.refs_0_
  99.1 0.2 convolution_convert_fusion.7
  99.3 0.2 copy.41.refs_1_
  99.5 0.2 convolution_convert_fusion.6
  99.7 0.2 copy.42.refs_2_
  99.9 4.0 %shard_map.95 = bf16[6912,128]{1,0:T(8,128)(2,1)S(1)} custom-call(bf16[576,576]{1,0:T(8,128)(2,1)S(1)} %convolution_convert_fusion.4.refs_0_, bf16[576,192]{1,0:T(8,128)(2,1)S(1)} %copy.41.refs_1_, bf16[576,192]{1,0:T(8,128)(2,1)S(1)} %copy.42.refs_2_, bf16[576,576]{1,0:T(8,128)(2,1)S(1)} %convolution_convert_fusion.3.refs_3_), custom_call_target="tpu_custom_call" | custom-call | tf_op jit(solution)/shard_map/pallas_call | solution.py:485
  103.9 2.5 %copy-done.1 = bf16[20736,128]{1,0:T(8,128)(2,1)S(1)} copy-done((bf16[20736,128]{1,0:T(8,128)(2,1)S(1)}, bf16[20736,128]{1,0:T(8,128)(2,1)}, u32[]{:S(2)}) %copy-start.1) | copy-done | bytes 5308440
  106.4 47.7 %shard_map.97 = (f32[3,72,128]{2,1,0:T(8,128)S(1)}, f32[9,72,128]{2,1,0:T(8,128)S(1)}, f32[2,576]{1,0:T(2,128)S(1)}) custom-call(bf16[2,2,2,2,2,3,72,128]{7,6,5,4,3,2,1,0:T(8,128)(2,1)S(1)} %bitcast.130, bf16[2,2,2,2,2,9,72,128]{7,6,5,4,3,2,1,0:T(8,128)(2,1)S(1)} %bitcast.129, f32[2,576]{1,0:T(2,128)S(1)} %pad_maximum_fusion.5.refs_2_), custom_call_target="tpu_custom_call" | custom-call | tf_op jit(solution)/shard_map/pallas_call | solution.py:594
  154.2 0.9 multiply_add_fusion
  155.1 0.7 copy-done.5
  155.9 1.4 convolution_add_fusion.3
  157.3 0.7 copy.56
  157.9 0.7 copy.57
  158.7 0.6 copy.58
  (88 shorter events, 0.6 us)
Async XLA Ops:
  3.7 0.9 copy-start.6
  4.7 0.8 copy-start.7
  57.1 0.7 copy-start.35
  57.1 1.1 copy-start.37
  57.4 1.1 copy-start.39
  57.5 1.1 copy-start.41
  58.5 1.0 copy-start.10
  59.3 0.9 copy-start.19
  60.1 9.2 %copy-start.8 = (f32[192,576]{1,0:T(8,128)}, f32[192,576]{1,0:T(8,128)S(1)}, u32[]{:S(2)}) copy-start(f32[192,576]{1,0:T(8,128)S(1)} %get-tuple-element.52) | copy-start | bytes 1327108
  60.2 4.3 %copy-start.15 = (bf16[192,576]{1,0:T(8,128)(2,1)}, bf16[192,576]{1,0:T(8,128)(2,1)S(1)}, u32[]{:S(2)}) copy-start(bf16[192,576]{1,0:T(8,128)(2,1)S(1)} %multiply_convert_fusion.3) | copy-start | bytes 663556
  63.8 1.3 copy-start.4
  64.5 1.1 copy-start.29
  67.4 1.8 %copy-start.22 = (bf16[192,1536]{1,0:T(8,128)(2,1)}, bf16[192,1536]{1,0:T(8,128)(2,1)S(1)}, u32[]{:S(2)}) copy-start(bf16[192,1536]{1,0:T(8,128)(2,1)S(1)} %get-tuple-element.35) | copy-start | bytes 1769476
  67.4 1.8 %copy-start.26 = (bf16[192,1536]{1,0:T(8,128)(2,1)}, bf16[192,1536]{1,0:T(8,128)(2,1)S(1)}, u32[]{:S(2)}) copy-start(bf16[192,1536]{1,0:T(8,128)(2,1)S(1)} %get-tuple-element.36) | copy-start | bytes 1769476
  69.4 0.8 copy-start.13
  74.6 0.8 copy-start.40
  74.7 0.8 copy-start.42
  75.5 0.9 copy-start.36
  75.5 1.0 copy-start.38
  75.8 2.0 %copy-start.21 = (bf16[192,576]{0,1:T(8,128)(2,1)S(1)}, bf16[192,576]{0,1:T(8,128)(2,1)}, u32[]{:S(2)}) copy-start(bf16[192,576]{0,1:T(8,128)(2,1)} %copy.37) | copy-start | bytes 663556
  75.9 2.7 %copy-start.17 = (bf16[1,192,9,64]{1,3,2,0:T(8,128)(2,1)}, bf16[1,192,9,64]{1,3,2,0:T(8,128)(2,1)S(1)}, u32[]{:S(2)}) copy-start(bf16[1,192,9,64]{1,3,2,0:T(8,128)(2,1)S(1)} %pad_maximum_fusion.1) | copy-start | bytes 663556
  76.9 0.6 copy-start.33
  77.6 1.4 copy-start.11
  78.3 0.6 copy-start.31
  78.3 2.0 %copy-start.16 = (bf16[192,576]{1,0:T(8,128)(2,1)S(1)}, bf16[192,576]{1,0:T(8,128)(2,1)}, u32[]{:S(2)}) copy-start(bf16[192,576]{1,0:T(8,128)(2,1)} %copy-done.15) | copy-start | bytes 663556
  78.3 2.0 %copy-start.23 = (bf16[192,1536]{1,0:T(8,128)(2,1)S(1)}, bf16[192,1536]{1,0:T(8,128)(2,1)}, u32[]{:S(2)}) copy-start(bf16[192,1536]{1,0:T(8,128)(2,1)} %copy-done.22) | copy-start | bytes 1769476
  80.3 2.0 %copy-start.27 = (bf16[192,1536]{1,0:T(8,128)(2,1)S(1)}, bf16[192,1536]{1,0:T(8,128)(2,1)}, u32[]{:S(2)}) copy-start(bf16[192,1536]{1,0:T(8,128)(2,1)} %copy-done.26) | copy-start | bytes 1769476
  82.2 1.9 %copy-start.24 = (bf16[192,1536]{1,0:T(8,128)(2,1)S(1)}, bf16[192,1536]{1,0:T(8,128)(2,1)}, u32[]{:S(2)}) copy-start(bf16[192,1536]{1,0:T(8,128)(2,1)} %get-tuple-element.37) | copy-start | bytes 1769476
  82.2 1.9 %copy-start.30 = (f32[192,576]{1,0:T(8,128)S(1)}, f32[192,576]{1,0:T(8,128)}, u32[]{:S(2)}) copy-start(f32[192,576]{1,0:T(8,128)} %param.6) | copy-start | bytes 1327108
  88.8 1.5 copy-start.2
  90.2 1.5 copy-start.3
  91.7 6.5 %copy-start.14 = (f32[192,576]{1,0:T(8,128)S(1)}, f32[192,576]{1,0:T(8,128)}, u32[]{:S(2)}) copy-start(f32[192,576]{1,0:T(8,128)} %copy-done.13) | copy-start | bytes 1327108
  91.7 6.5 %copy-start.20 = (bf16[3,64,3,192]{3,1,2,0:T(8,128)(2,1)S(1)}, bf16[3,64,3,192]{3,1,2,0:T(8,128)(2,1)}, u32[]{:S(2)}) copy-start(bf16[3,64,3,192]{3,1,2,0:T(8,128)(2,1)} %copy-done.19) | copy-start | bytes 663556
  91.7 6.9 %copy-start.18 = (bf16[1,192,9,64]{1,3,2,0:T(8,128)(2,1)S(1)}, bf16[1,192,9,64]{1,3,2,0:T(8,128)(2,1)}, u32[]{:S(2)}) copy-start(bf16[1,192,9,64]{1,3,2,0:T(8,128)(2,1)} %copy-done.17) | copy-start | bytes 663556
  95.8 2.3 %copy-start = (bf16[20736,128]{1,0:T(8,128)(2,1)}, bf16[20736,128]{1,0:T(8,128)(2,1)S(1)}, u32[]{:S(2)}) copy-start(bf16[20736,128]{1,0:T(8,128)(2,1)S(1)} %shard_map.96) | copy-start | bytes 15925252
  98.2 0.9 copy-start.34
  98.2 1.3 copy-start.32
  103.9 2.5 %copy-start.1 = (bf16[20736,128]{1,0:T(8,128)(2,1)S(1)}, bf16[20736,128]{1,0:T(8,128)(2,1)}, u32[]{:S(2)}) copy-start(bf16[20736,128]{1,0:T(8,128)(2,1)} %copy-done) | copy-start | bytes 15925252
  106.4 47.8 %copy-start.12 = (f32[192,576]{1,0:T(8,128)S(1)}, f32[192,576]{1,0:T(8,128)}, u32[]{:S(2)}) copy-start(f32[192,576]{1,0:T(8,128)} %param.5) | copy-start | bytes 1327108
  106.4 47.8 %copy-start.28 = (f32[192,576]{1,0:T(8,128)S(1)}, f32[192,576]{1,0:T(8,128)}, u32[]{:S(2)}) copy-start(f32[192,576]{1,0:T(8,128)} %get-tuple-element.56) | copy-start | bytes 1327108
  106.4 48.7 %copy-start.9 = (f32[192,576]{1,0:T(8,128)S(1)}, f32[192,576]{1,0:T(8,128)}, u32[]{:S(2)}) copy-start(f32[192,576]{1,0:T(8,128)} %copy-done.8) | copy-start | bytes 1327108
  106.4 48.7 %copy-start.25 = (bf16[192,1536]{1,0:T(8,128)(2,1)S(1)}, bf16[192,1536]{1,0:T(8,128)(2,1)}, u32[]{:S(2)}) copy-start(bf16[192,1536]{1,0:T(8,128)(2,1)} %get-tuple-element.37) | copy-start | bytes 1769476
  154.1 1.7 %copy-start.5 = (bf16[1536,576]{1,0:T(8,128)(2,1)S(1)}, bf16[1536,576]{1,0:T(8,128)(2,1)}, u32[]{:S(2)}) copy-start(bf16[1536,576]{1,0:T(8,128)(2,1)} %copy-done.4) | copy-start | bytes 5308420
